TPU v7x, 512 devices: a whole 4x8x8 slice. The times are simulated.
512 devices in a mesh: row: 32 (over z, x_lo, core), col: 16 (over y, x_hi).
Axes of the slice: x: 4 (x_hi: 2, x_lo: 2; x = x_hi * 2 + x_lo), y: 8, z: 8, core: 2. Of those that a mesh axis runs over, the one named last changes fastest.
Arguments:
- amplitudes: float32 [8192, 8192], P('row', 'col'), may hold values from -6 to 6
- factor: float32 [8192, 512], P('col'), may hold values from -1.2 to 1.2
- denominators: float32 [8192, 8192], P('row', 'col'), may hold values from 1 to 4
Outputs:
- new_amplitudes: float32 [8192, 8192], P('row', 'col')
All inputs are finite; a program needn't handle non-finite values.
Results may differ from a plain program's by a relative error of at most 0.0001.
Values sent between devices are 32-bit elements; how exact they have to be, the bound alone decides.
No kernel may reach another device: no remote copies, remote signals or barrier semaphores. Data moves between devices by JAX's collectives and lax.ppermute only.
A program may use at most 64 MiB of HBM per device.

v0:
```python
import math

import jax
import jax.numpy as jnp
from jax import lax
from jax.sharding import PartitionSpec as P

ITERS = 2


def broadcast(value, axis, source):
    kept = jnp.where(lax.axis_index(axis) == source, value, 0).astype(value.dtype)
    return lax.psum(kept, axis)


def inner(left, right):
    return lax.dot_general(left, right, (((1,), (1,)), ((), ())), precision=lax.Precision.HIGHEST)


def local(amplitudes, factor, denominators):
    high = lax.Precision.HIGHEST
    rows = amplitudes.shape[0]
    nrow = lax.axis_size("row")
    ratio = nrow // lax.axis_size("col")
    here_row = lax.axis_index("row")
    here_col = lax.axis_index("col")
    scale = 1.0 / math.sqrt(rows * nrow)
    mine = lax.dynamic_slice_in_dim(factor, here_row % ratio * rows, rows, 0)
    factor_rows = broadcast(mine, "col", here_row // ratio)
    base = inner(factor_rows, factor)
    amp = amplitudes
    for step in range(ITERS):
        partial_value = jnp.dot(amp, factor, precision=high)
        y_rows = lax.psum(partial_value, "col") * scale
        pieces = []
        for extra in range(ratio):
            pieces.append(broadcast(y_rows, "row", here_col * ratio + extra))
        y_cols = jnp.concatenate(pieces, axis=0)
        result = base + inner(y_rows, y_cols) + inner(y_rows, factor) + inner(factor_rows, y_cols)
        amp = result / denominators
    return amp


def solution(mesh):
    return jax.shard_map(
        local,
        mesh=mesh,
        in_specs=(P("row", "col"), P("col", None), P("row", "col")),
        out_specs=P("row", "col"),
        check_vma=False,
    )
```

profile of v0, /device:TPU:1, one launch (start us, length us, event | category | flops | bytes accessed | tf_op | source)
XLA Modules:
  0.0 842.6 jit_solution(15088821909346795326)
XLA Ops:
  6.5 0.0 copy-start
  6.5 0.0 all-reduce.14.cloned.1.call-start
  6.5 1.0 copy-done
  7.6 0.0 copy-start.1
  7.6 3.2 fusion.15
  10.8 0.0 copy-done.1
  10.8 0.8 dynamic-slice_select_fusion
  11.6 0.0 all-reduce.14.cloned.1.call-update
  11.6 0.0 all-reduce.12.cloned.1.call-start
  11.7 161.4 %all-reduce.14.cloned.1.call-done = (f32[256,512]{1,0:T(8,128)}, f32[256,512]{1,0:T(8,128)}) async-done(((f32[256,512]{1,0:T(8,128)}, f32[256,512]{1,0:T(8,128)}), (f32[256,512]{1,0:T(8,128)}, f32[256,512]{1,0:T(8,128)})) %all-reduce.14.cloned.1.call-update) | async-done | bytes 1048592 | tf_op jit(solution)/shard_map/psum | solution.py:13
  173.1 2.2 multiply_select_fusion.2
  175.3 0.0 copy-start.4
  175.3 0.0 all-reduce.12.cloned.1.call-update
  175.3 0.0 all-reduce.8.cloned.1.call-start
  175.4 1.0 copy-done.4
  176.3 1.0 fusion.14
  177.4 243.6 %all-reduce.12.cloned.1.call-done = (f32[256,512]{1,0:T(8,128)}, f32[256,512]{1,0:T(8,128)}) async-done(((f32[256,512]{1,0:T(8,128)}, f32[256,512]{1,0:T(8,128)}), (f32[256,512]{1,0:T(8,128)}, f32[256,512]{1,0:T(8,128)})) %all-reduce.12.cloned.1.call-update) | async-done | bytes 1048592 | tf_op jit(solution)/shard_map/psum | solution.py:13
  421.0 0.0 copy-start.6
  421.0 1.1 constant_dynamic-update-slice_fusion.1
  422.1 0.1 copy-done.6
  422.2 0.0 copy-start.2
  422.2 1.0 copy-done.2
  423.2 1.1 convolution_add_fusion.5
  424.3 0.0 copy-start.5
  424.3 1.1 convolution_add_fusion.4
  425.4 0.0 copy-done.5
  425.4 1.1 fusion
  426.5 1.8 fusion.16
  428.3 0.0 all-reduce.8.cloned.1.call-update
  428.4 0.0 all-reduce.10.cloned.1.call-start
  428.4 153.1 %all-reduce.8.cloned.1.call-done = f32[256,512]{1,0:T(8,128)} async-done(((f32[256,512]{1,0:T(8,128)}), f32[256,512]{1,0:T(8,128)}) %all-reduce.8.cloned.1.call-update) | async-done | bytes 524304 | tf_op jit(solution)/shard_map/psum | solution.py:34
  581.5 2.2 multiply_select_fusion
  583.7 0.0 all-reduce.10.cloned.1.call-update
  583.7 246.1 %all-reduce.10.cloned.1.call-done = (f32[256,512]{1,0:T(8,128)}, f32[256,512]{1,0:T(8,128)}) async-done(((f32[256,512]{1,0:T(8,128)}, f32[256,512]{1,0:T(8,128)}), (f32[256,512]{1,0:T(8,128)}, f32[256,512]{1,0:T(8,128)})) %all-reduce.10.cloned.1.call-update) | async-done | bytes 1048592 | tf_op jit(solution)/shard_map/psum | solution.py:13
  829.8 0.0 copy-start.7
  829.8 1.1 constant_dynamic-update-slice_fusion.3
  831.0 0.1 copy-done.7
  831.0 0.0 copy-start.3
  831.1 1.0 copy-done.3
  832.1 1.1 convolution_add_fusion.2
  833.2 1.1 convolution_add_fusion.1
  834.2 1.9 fusion.1
  (2 shorter events, 0.1 us)
Async XLA Ops:
  6.5 1.0 copy-start
  6.5 166.6 %all-reduce.14.cloned.1.call-start = ((), (), s32[]{:S(2)}) async-start(), calls=%async_computation.3 | async-start | bytes 2097152 | tf_op jit(solution)/shard_map/psum | solution.py:13
  7.6 3.2 copy-start.1
  11.6 409.4 %all-reduce.12.cloned.1.call-start = ((), (), s32[]{:S(2)}) async-start(), calls=%async_computation.2 | async-start | bytes 2097152 | tf_op jit(solution)/shard_map/psum | solution.py:13
  175.3 1.0 copy-start.4
  175.3 406.2 %all-reduce.8.cloned.1.call-start = ((), (), s32[]{:S(2)}) async-start(), calls=%async_computation | async-start | bytes 1048576 | tf_op jit(solution)/shard_map/psum | solution.py:34
  421.0 1.2 copy-start.6
  422.2 1.0 copy-start.2
  424.3 1.1 copy-start.5
  428.4 401.5 %all-reduce.10.cloned.1.call-start = ((), (), s32[]{:S(2)}) async-start(), calls=%async_computation.1 | async-start | bytes 2097152 | tf_op jit(solution)/shard_map/psum | solution.py:13
  829.8 1.2 copy-start.7
  831.0 1.0 copy-start.3
Sparse Core Ops, SparseCore 0:
  11.7 161.3 all-reduce.13
  176.1 244.9 all-reduce.11
  428.5 152.9 all-reduce.7
  584.3 245.4 all-reduce.9
where the time goes:
time: 843 us
  waiting for transfers between devices  804 us (95%)
  matrix products  13.3 us (2%)
  between operations  13.2 us (2%)
    psum x3, waiting for transfers between devices, broadcast(): return lax.psum(kept, axis)  651 us
    psum x1, waiting for transfers between devices, local(): y_rows = lax.psum(partial_value, 'col') * scale  153 us
  transfers between devices with their start and end apart: 4, of which 4 were waited for; matrix products, arithmetic and copies ran while one was open for 0% of the time, Pallas kernels for 0%

commit v1 on v0

v1 whole, which is shorter than its diff:
```python
import math

import jax
import jax.numpy as jnp
from jax import lax
from jax.sharding import PartitionSpec as P

ITERS = 2
PRECISION = lax.Precision.HIGH


def spread(block, axis, groups=None):
    return lax.all_to_all(block, axis, split_axis=0, concat_axis=0, axis_index_groups=groups, tiled=True)


def local(amplitudes, factor, denominators):
    rows, depth = amplitudes.shape[0], factor.shape[1]
    nrow = lax.axis_size("row")
    ncol = lax.axis_size("col")
    ratio = nrow // ncol
    here_row = lax.axis_index("row")
    here_col = lax.axis_index("col")
    scale = 1.0 / math.sqrt(rows * nrow)
    mine = lax.dynamic_slice_in_dim(factor, here_row % ratio * rows, rows, 0)
    mine = jnp.where(here_row // ratio == here_col, mine, 0.0)
    apart = [[k * ratio + e for k in range(ncol)] for e in range(ratio)]
    team = [[k * ratio + e for e in range(ratio)] for k in range(ncol)]
    turn = []
    for k in range(ncol):
        for e in range(ratio):
            for c in range(ncol):
                turn.append(((k * ratio + e) * ncol + c, (c * ratio + e) * ncol + k))
    amp = amplitudes
    for step in range(ITERS):
        part = jnp.dot(amp, factor, precision=PRECISION) * scale + mine
        terms = spread(part, "col")
        piece = terms.reshape(ncol, rows // ncol, depth).sum(0)
        turned = lax.ppermute(piece, ("row", "col"), turn)
        z_rows = spread(jnp.tile(piece, (ncol, 1)), "col")
        turned, z_rows = lax.optimization_barrier((turned, z_rows))
        z_half = spread(jnp.tile(turned, (ncol, 1)), "row", apart)
        z_cols = spread(jnp.tile(z_half, (ratio, 1)), "row", team)
        full = lax.dot_general(z_rows, z_cols, (((1,), (1,)), ((), ())), precision=PRECISION)
        amp = full / denominators
    return amp


def solution(mesh):
    return jax.shard_map(
        local,
        mesh=mesh,
        in_specs=(P("row", "col"), P("col", None), P("row", "col")),
        out_specs=P("row", "col"),
        check_vma=False,
    )
```

time: 843 us -> 169 us (0.20)
  waiting for transfers between devices: 804 us -> 32.7 us
  blocking collectives: 0 us -> 117 us
  between operations: 13.2 us -> 0.12 us
  starting transfers between devices: 0.13 us -> 10.5 us
  matrix products: 13.3 us -> 4.65 us
    psum x4 -> x0, waiting for transfers between devices: 804 us -> none  [the longest x3 651 us: broadcast(): return lax.psum(kept, axis)]
    all_to_all x0 -> x6, blocking collectives: none -> 117 us  [spread(): lax.all_to_all(block, axis, split_axis=0, concat_axis=0, axis_index_group...]
    all_to_all x0 -> x2, waiting for transfers between devices: none -> 32.7 us  [spread(): lax.all_to_all(block, axis, split_axis=0, concat_axis=0, axis_index_group...]
    all_to_all x0 -> x2, starting transfers between devices: none -> 9.16 us  [spread(): lax.all_to_all(block, axis, split_axis=0, concat_axis=0, axis_index_group...]
    dot_general x9 -> x4, matrix products: 13.3 us -> 4.65 us  [the longest x2 2.59 us: local(): part = jnp.dot(amp, factor, precision=PRECISION) * scale + mine]
  transfers between devices with their start and end apart: 4 -> 4, of which waited for: 4 -> 2; matrix products, arithmetic and copies ran while one was open for 0% -> 0% of each run, Pallas kernels for 0% -> 0%
where the time goes in v1:
time: 169 us; the launch traced here: 168 us
  blocking collectives  117 us (69%)
  waiting for transfers between devices  32.7 us (19%)
  starting transfers between devices  10.5 us (6%)
  matrix products  4.65 us (3%)
  local copies, waits for them, and re-layouts  3.68 us (2%)
    all_to_all x6, blocking collectives, spread(): lax.all_to_all(block, axis, split_axis=0, concat_axis=0, axis_index_group...  117 us
    all_to_all x2, waiting for transfers between devices, spread(): lax.all_to_all(block, axis, split_axis=0, concat_axis=0, axis_index_group...  32.7 us
    all_to_all x2, starting transfers between devices, spread(): lax.all_to_all(block, axis, split_axis=0, concat_axis=0, axis_index_group...  9.16 us
  transfers between devices with their start and end apart: 4, of which 2 were waited for; matrix products, arithmetic and copies ran while one was open for 0% of the time, Pallas kernels for 0%

profile of v1, /device:TPU:1, one launch (start us, length us, event | category | flops | bytes accessed | tf_op | source)
XLA Modules:
  0.0 168.4 jit_solution(943852700777565701)
XLA Ops:
  0.0 0.0 copy-start
  0.0 1.0 copy-done
  1.0 2.0 %fusion = f32[256,512]{1,0:T(8,128)S(1)} fusion(f32[256,512]{1,0:T(8,128)S(1)} %copy-done, f32[512,512]{1,0:T(8,128)} %param.4, s32[]{:T(128)S(6)} %select_n.25, pred[]{:T(512)S(6)} %eq.5), kind=kOutput, calls=%fused_computation.4 | convolution fusion | flops 403046400 | bytes 2621445 | tf_op jit(solution)/shard_map/dot_general | solution.py:35
  3.0 27.2 %all_to_all.66 = f32[16,16,512]{2,1,0:T(8,128)S(1)} all-to-all(f32[16,16,512]{2,1,0:T(8,128)S(1)} %bitcast.23), channel_id=1, replica_groups=mesh['row'=32,'col'=16] {'col'}, dimensions={0} | all-to-all | bytes 1048576 | tf_op jit(solution)/shard_map/all_to_all | solution.py:13
  30.3 0.9 tile.16
  31.1 4.7 %all-to-all-start.1 = ((f32[16,16,512]{2,1,0:T(8,128)}), f32[16,16,512]{2,1,0:T(8,128)S(1)}, u32[]{:S(2)}, u32[]{:S(2)}) async-start(f32[16,16,512]{2,1,0:T(8,128)} %tile.16), calls=%async_computation.1 | async-start | bytes 1048576 | tf_op jit(solution)/shard_map/all_to_all | solution.py:13
  35.9 0.7 collective-permute-start
  36.5 0.0 collective-permute-done
  36.5 16.7 %all-to-all-done.1 = f32[16,16,512]{2,1,0:T(8,128)S(1)} async-done(((f32[16,16,512]{2,1,0:T(8,128)}), f32[16,16,512]{2,1,0:T(8,128)S(1)}, u32[]{:S(2)}, u32[]{:S(2)}) %all-to-all-start.1) | async-done | bytes 524320 | tf_op jit(solution)/shard_map/all_to_all | solution.py:13
  53.3 21.9 %all_to_all.67 = f32[16,16,512]{2,1,0:T(8,128)S(1)} all-to-all(f32[16,16,512]{2,1,0:T(8,128)S(1)} %tile.17), channel_id=1, replica_groups={{0,32,64,96,128,160,192,224,256,288,320,352,384,416,448,480},{16,48,80,..., dimensions={0} | all-to-all | bytes 1048576 | tf_op jit(solution)/shard_map/all_to_all | solution.py:13
  75.3 0.1 tile.19
  75.4 0.0 copy-start.2
  75.4 10.6 %all_to_all.68 = f32[2,256,512]{2,1,0:T(8,128)S(1)} all-to-all(f32[2,256,512]{2,1,0:T(8,128)S(1)} %tile.19), channel_id=1, replica_groups={{0,16},{32,48},{64,80},{96,112},{128,144},{160,176},{192,208},{224,240}..., dimensions={0} | all-to-all | bytes 2097152 | tf_op jit(solution)/shard_map/all_to_all | solution.py:13
  86.0 0.0 copy-done.2
  86.0 0.0 copy-start.1
  86.0 0.6 convolution_divide_fusion.1
  86.7 0.6 copy-done.1
  87.3 0.6 fusion.1
  87.9 25.4 %all_to_all.69 = f32[16,16,512]{2,1,0:T(8,128)S(1)} all-to-all(f32[16,16,512]{2,1,0:T(8,128)S(1)} %bitcast.22), channel_id=1, replica_groups=mesh['row'=32,'col'=16] {'col'}, dimensions={0} | all-to-all | bytes 1048576 | tf_op jit(solution)/shard_map/all_to_all | solution.py:13
  113.3 0.9 tile.20
  114.1 4.4 %all-to-all-start.5 = ((f32[16,16,512]{2,1,0:T(8,128)}), f32[16,16,512]{2,1,0:T(8,128)S(1)}, u32[]{:S(2)}, u32[]{:S(2)}) async-start(f32[16,16,512]{2,1,0:T(8,128)} %tile.20), calls=%async_computation.5 | async-start | bytes 1048576 | tf_op jit(solution)/shard_map/all_to_all | solution.py:13
  118.6 0.7 collective-permute-start.1
  119.3 0.0 collective-permute-done.1
  119.3 16.0 %all-to-all-done.5 = f32[16,16,512]{2,1,0:T(8,128)S(1)} async-done(((f32[16,16,512]{2,1,0:T(8,128)}), f32[16,16,512]{2,1,0:T(8,128)S(1)}, u32[]{:S(2)}, u32[]{:S(2)}) %all-to-all-start.5) | async-done | bytes 524320 | tf_op jit(solution)/shard_map/all_to_all | solution.py:13
  135.3 23.6 %all_to_all.70 = f32[16,16,512]{2,1,0:T(8,128)S(1)} all-to-all(f32[16,16,512]{2,1,0:T(8,128)S(1)} %tile.21), channel_id=1, replica_groups={{0,32,64,96,128,160,192,224,256,288,320,352,384,416,448,480},{16,48,80,..., dimensions={0} | all-to-all | bytes 1048576 | tf_op jit(solution)/shard_map/all_to_all | solution.py:13
  158.9 0.1 tile.23
  159.0 8.0 %all_to_all.71 = f32[2,256,512]{2,1,0:T(8,128)S(1)} all-to-all(f32[2,256,512]{2,1,0:T(8,128)S(1)} %tile.23), channel_id=1, replica_groups={{0,16},{32,48},{64,80},{96,112},{128,144},{160,176},{192,208},{224,240}..., dimensions={0} | all-to-all | bytes 2097152 | tf_op jit(solution)/shard_map/all_to_all | solution.py:13
  167.0 1.4 convolution_divide_fusion
  (4 shorter events, 0.2 us)
Async XLA Ops:
  0.0 1.0 copy-start
  31.1 22.2 %all-to-all-start.1 = ((f32[16,16,512]{2,1,0:T(8,128)}), f32[16,16,512]{2,1,0:T(8,128)S(1)}, u32[]{:S(2)}, u32[]{:S(2)}) async-start(f32[16,16,512]{2,1,0:T(8,128)} %tile.16), calls=%async_computation.1 | async-start | bytes 1048576 | tf_op jit(solution)/shard_map/all_to_all | solution.py:13
  35.9 0.7 collective-permute-start
  75.4 10.7 %copy-start.2 = (f32[256,512]{1,0:T(8,128)S(1)}, f32[256,512]{1,0:T(8,128)}, u32[]{:S(2)}) copy-start(f32[256,512]{1,0:T(8,128)} %param.5) | copy-start | bytes 1572868
  86.0 1.2 copy-start.1
  114.1 21.1 %all-to-all-start.5 = ((f32[16,16,512]{2,1,0:T(8,128)}), f32[16,16,512]{2,1,0:T(8,128)S(1)}, u32[]{:S(2)}, u32[]{:S(2)}) async-start(f32[16,16,512]{2,1,0:T(8,128)} %tile.20), calls=%async_computation.5 | async-start | bytes 1048576 | tf_op jit(solution)/shard_map/all_to_all | solution.py:13
  118.6 0.7 collective-permute-start.1

commit v2 on v1

v2 whole, which is shorter than its diff:
```python
import math

import jax
import jax.numpy as jnp
from jax import lax
from jax.sharding import PartitionSpec as P

ITERS = 2
PRECISION = lax.Precision.HIGH
PAIR = 2
CORES = 2


def spread(block, axis, groups):
    return lax.all_to_all(block, axis, split_axis=0, concat_axis=0, axis_index_groups=groups, tiled=True)


def ordered(first, second, swapped):
    return jnp.where(swapped, jnp.concatenate([second, first]), jnp.concatenate([first, second]))


def local(amplitudes, factor, denominators):
    rows, depth = amplitudes.shape[0], factor.shape[1]
    nrow = lax.axis_size("row")
    ncol = lax.axis_size("col")
    line = ncol // PAIR
    here_row = lax.axis_index("row")
    here_col = lax.axis_index("col")
    scale = 1.0 / math.sqrt(rows * nrow)
    mine = lax.dynamic_slice_in_dim(factor, here_row % CORES * rows, rows, 0)
    mine = jnp.where(here_row // CORES == here_col, mine, 0.0)
    along_y = [[y * PAIR + u for y in range(line)] for u in range(PAIR)]
    along_z = [[z * PAIR * CORES + q for z in range(line)] for q in range(PAIR * CORES)]
    team = [[k * CORES + e for e in range(CORES)] for k in range(nrow // CORES)]
    across = [(c, c ^ 1) for c in range(ncol)]
    turns = [[], []]
    for r in range(nrow):
        for c in range(ncol):
            j = c % PAIR * line + c // PAIR
            for t in range(PAIR):
                to = (j // PAIR * PAIR + (j % PAIR ^ t)) * CORES + r % CORES
                turns[t].append((r * ncol + c, to * ncol + r // CORES))
    odd_u = here_col % PAIR == 1
    odd_v = here_row // CORES % PAIR == 1
    amp = amplitudes
    for step in range(ITERS):
        part = jnp.dot(amp, factor, precision=PRECISION) * scale + mine
        terms = spread(part, "col", [sum(along_y, [])])
        piece = terms.reshape(ncol, rows // ncol, depth).sum(0)
        near = lax.ppermute(piece, ("row", "col"), turns[0])
        far = lax.ppermute(piece, ("row", "col"), turns[1])
        row_half = spread(jnp.tile(piece, (line, 1)), "col", along_y)
        row_rest = lax.ppermute(row_half, "col", across)
        two = ordered(near, far, odd_v)
        col_half = spread(jnp.tile(two, (line, 1)), "row", along_z)
        z_cols = spread(jnp.tile(col_half, (CORES, 1)), "row", team)
        z_rows = ordered(row_half, row_rest, odd_u)
        full = lax.dot_general(z_rows, z_cols, (((1,), (1,)), ((), ())), precision=PRECISION)
        amp = full / denominators
    return amp


def solution(mesh):
    return jax.shard_map(
        local,
        mesh=mesh,
        in_specs=(P("row", "col"), P("col", None), P("row", "col")),
        out_specs=P("row", "col"),
        check_vma=False,
    )
```

time: 169 us -> 172 us (1.018)
  blocking collectives: 117 us -> 49.1 us
  starting transfers between devices: 10.5 us -> 70.6 us
  waiting for transfers between devices: 32.7 us -> 39.8 us
  local copies, waits for them, and re-layouts: 3.68 us -> 7.01 us
    all_to_all x6 -> x2, blocking collectives: 117 us -> 49.1 us  [spread(): lax.all_to_all(block, axis, split_axis=0, concat_axis=0, axis_index_group...]
    all_to_all x2 -> x6, starting transfers between devices: 9.16 us -> 58.7 us  [spread(): lax.all_to_all(block, axis, split_axis=0, concat_axis=0, axis_index_group...]
    ppermute x2 -> x6, starting transfers between devices: 1.33 us -> 12 us  [the longest x2 6.04 us: local(): row_rest = lax.ppermute(row_half, 'col', across)]
    ppermute x2 -> x6, waiting for transfers between devices: 0.01 us -> 6.09 us  [the longest x2 6.08 us: local(): far = lax.ppermute(piece, ('row', 'col'), turns[1])]
    another operation x6, local copies, waits for them, and re-layouts: 2.05 us -> 5.38 us  [the longest x2 2.21 us: local(): z_cols = spread(jnp.tile(col_half, (CORES, 1)), 'row', team)]
    all_to_all x2 -> x6, waiting for transfers between devices: 32.7 us -> 33.7 us  [spread(): lax.all_to_all(block, axis, split_axis=0, concat_axis=0, axis_index_group...]
  transfers between devices with their start and end apart: 4 -> 12, of which waited for: 2 -> 8; matrix products, arithmetic and copies ran while one was open for 0% -> 1% of each run, Pallas kernels for 0% -> 0%
where the time goes in v2:
time: 172 us; the launch traced here: 171 us
  starting transfers between devices  70.6 us (41%)
  blocking collectives  49.1 us (29%)
  waiting for transfers between devices  39.8 us (23%)
  local copies, waits for them, and re-layouts  7.01 us (4%)
  matrix products  4.65 us (3%)
    all_to_all x6, starting transfers between devices, spread(): lax.all_to_all(block, axis, split_axis=0, concat_axis=0, axis_index_group...  58.7 us
    all_to_all x2, blocking collectives, spread(): lax.all_to_all(block, axis, split_axis=0, concat_axis=0, axis_index_group...  49.1 us
    all_to_all x6, waiting for transfers between devices, spread(): lax.all_to_all(block, axis, split_axis=0, concat_axis=0, axis_index_group...  33.7 us
    ppermute x2, waiting for transfers between devices, local(): far = lax.ppermute(piece, ('row', 'col'), turns[1])  6.08 us
    ppermute x2, starting transfers between devices, local(): row_rest = lax.ppermute(row_half, 'col', across)  6.04 us
    ppermute x2, starting transfers between devices, local(): far = lax.ppermute(piece, ('row', 'col'), turns[1])  4.61 us
  transfers between devices with their start and end apart: 12, of which 8 were waited for; matrix products, arithmetic and copies ran while one was open for 1% of the time, Pallas kernels for 0%

profile of v2, /device:TPU:1, one launch (start us, length us, event | category | flops | bytes accessed | tf_op | source)
XLA Modules:
  0.0 171.3 jit_solution(6625545493360262828)
XLA Ops:
  0.0 0.0 copy-start
  0.0 1.0 copy-done
  1.0 2.0 %fusion = f32[256,512]{1,0:T(8,128)S(1)} fusion(f32[256,512]{1,0:T(8,128)S(1)} %copy-done, f32[512,512]{1,0:T(8,128)} %param.4, s32[]{:T(128)S(6)} %select_n.68, pred[]{:T(512)S(6)} %eq.14), kind=kOutput, calls=%fused_computation.4 | convolution fusion | flops 403046400 | bytes 2621445 | tf_op jit(solution)/shard_map/dot_general | solution.py:47
  3.0 25.3 %all_to_all.66 = f32[16,16,512]{2,1,0:T(8,128)S(1)} all-to-all(f32[16,16,512]{2,1,0:T(8,128)S(1)} %bitcast.17), channel_id=1, replica_groups={{0,2,4,6,8,10,12,14,1,3,5,7,9,11,13,15},{16,18,20,22,24,26,28,30,17,19,..., dimensions={0} | all-to-all | bytes 1048576 | tf_op jit(solution)/shard_map/all_to_all | solution.py:15
  28.4 0.7 tile.16
  29.1 4.8 %all-to-all-start.1 = ((f32[8,16,512]{2,1,0:T(8,128)}), f32[8,16,512]{2,1,0:T(8,128)S(1)}, u32[]{:S(2)}, u32[]{:S(2)}) async-start(f32[8,16,512]{2,1,0:T(8,128)} %tile.16), calls=%async_computation.1 | async-start | bytes 524288 | tf_op jit(solution)/shard_map/all_to_all | solution.py:15
  33.9 2.2 %collective-permute-start.1 = (f32[16,512]{1,0:T(8,128)S(1)}, f32[16,512]{1,0:T(8,128)S(1)}, u32[]{:S(2)}, u32[]{:S(2)}) collective-permute-start(f32[16,512]{1,0:T(8,128)S(1)} %reduce_sum.18), channel_id=1, source_target_pairs={{0,32},{1,288},{2,0},{3,256},{4,96},{5,352},{6,64},{7,320},{8,160}... | collective-permute-start | bytes 98312 | tf_op jit(solution)/shard_map/ppermute | solution.py:51
  36.1 0.7 collective-permute-start.2
  36.8 2.2 %collective-permute-done.1 = f32[16,512]{1,0:T(8,128)S(1)} collective-permute-done((f32[16,512]{1,0:T(8,128)S(1)}, f32[16,512]{1,0:T(8,128)S(1)}, u32[]{:S(2)}, u32[]{:S(2)}) %collective-permute-start.1) | collective-permute-done | bytes 32800 | tf_op jit(solution)/shard_map/ppermute | solution.py:51
  39.0 0.0 collective-permute-done.2
  39.0 4.2 %all-to-all-done.1 = f32[8,16,512]{2,1,0:T(8,128)S(1)} async-done(((f32[8,16,512]{2,1,0:T(8,128)}), f32[8,16,512]{2,1,0:T(8,128)S(1)}, u32[]{:S(2)}, u32[]{:S(2)}) %all-to-all-start.1) | async-done | bytes 262176 | tf_op jit(solution)/shard_map/all_to_all | solution.py:15
  43.2 0.9 tile.17
  44.1 18.3 %all-to-all-start.2 = ((f32[8,32,512]{2,1,0:T(8,128)}), f32[8,32,512]{2,1,0:T(8,128)S(1)}, u32[]{:S(2)}, u32[]{:S(2)}) async-start(f32[8,32,512]{2,1,0:T(8,128)} %tile.17), calls=%async_computation.2 | async-start | bytes 1048576 | tf_op jit(solution)/shard_map/all_to_all | solution.py:15
  62.3 4.1 %collective-permute-start = (f32[128,512]{1,0:T(8,128)S(1)}, f32[128,512]{1,0:T(8,128)S(1)}, u32[]{:S(2)}, u32[]{:S(2)}) collective-permute-start(f32[128,512]{1,0:T(8,128)S(1)} %bitcast.20), channel_id=1, source_target_pairs={{0,1},{1,0},{2,3},{3,2},{4,5},{5,4},{6,7},{7,6},{8,9},{9,8},{10,11... | collective-permute-start | bytes 786440 | tf_op jit(solution)/shard_map/ppermute | solution.py:53
  66.5 10.7 %all-to-all-done.2 = f32[8,32,512]{2,1,0:T(8,128)S(1)} async-done(((f32[8,32,512]{2,1,0:T(8,128)}), f32[8,32,512]{2,1,0:T(8,128)S(1)}, u32[]{:S(2)}, u32[]{:S(2)}) %all-to-all-start.2) | async-done | bytes 524320 | tf_op jit(solution)/shard_map/all_to_all | solution.py:15
  77.2 1.1 tile.19
  78.3 0.0 copy-start.2
  78.3 7.3 %all-to-all-start.3 = ((f32[2,256,512]{2,1,0:T(8,128)}), f32[2,256,512]{2,1,0:T(8,128)S(1)}, u32[]{:S(2)}, u32[]{:S(2)}) async-start(f32[2,256,512]{2,1,0:T(8,128)} %tile.19), calls=%async_computation.3 | async-start | bytes 2097152 | tf_op jit(solution)/shard_map/all_to_all | solution.py:15
  85.6 0.0 collective-permute-done
  85.6 1.7 %all-to-all-done.3 = f32[2,256,512]{2,1,0:T(8,128)S(1)} async-done(((f32[2,256,512]{2,1,0:T(8,128)}), f32[2,256,512]{2,1,0:T(8,128)S(1)}, u32[]{:S(2)}, u32[]{:S(2)}) %all-to-all-start.3) | async-done | bytes 1048608 | tf_op jit(solution)/shard_map/all_to_all | solution.py:15
  87.4 0.0 copy-done.2
  87.4 0.0 copy-start.1
  87.4 0.6 convolution_divide_fusion.1
  88.0 0.6 copy-done.1
  88.6 0.6 fusion.1
  89.2 23.8 %all_to_all.67 = f32[16,16,512]{2,1,0:T(8,128)S(1)} all-to-all(f32[16,16,512]{2,1,0:T(8,128)S(1)} %bitcast.16), channel_id=1, replica_groups={{0,2,4,6,8,10,12,14,1,3,5,7,9,11,13,15},{16,18,20,22,24,26,28,30,17,19,..., dimensions={0} | all-to-all | bytes 1048576 | tf_op jit(solution)/shard_map/all_to_all | solution.py:15
  113.0 0.7 tile.20
  113.7 5.6 %all-to-all-start.5 = ((f32[8,16,512]{2,1,0:T(8,128)}), f32[8,16,512]{2,1,0:T(8,128)S(1)}, u32[]{:S(2)}, u32[]{:S(2)}) async-start(f32[8,16,512]{2,1,0:T(8,128)} %tile.20), calls=%async_computation.5 | async-start | bytes 524288 | tf_op jit(solution)/shard_map/all_to_all | solution.py:15
  119.3 2.4 %collective-permute-start.4 = (f32[16,512]{1,0:T(8,128)S(1)}, f32[16,512]{1,0:T(8,128)S(1)}, u32[]{:S(2)}, u32[]{:S(2)}) collective-permute-start(f32[16,512]{1,0:T(8,128)S(1)} %reduce_sum.19), channel_id=1, source_target_pairs={{0,32},{1,288},{2,0},{3,256},{4,96},{5,352},{6,64},{7,320},{8,160}... | collective-permute-start | bytes 98312 | tf_op jit(solution)/shard_map/ppermute | solution.py:51
  121.7 0.7 collective-permute-start.5
  122.4 3.9 %collective-permute-done.4 = f32[16,512]{1,0:T(8,128)S(1)} collective-permute-done((f32[16,512]{1,0:T(8,128)S(1)}, f32[16,512]{1,0:T(8,128)S(1)}, u32[]{:S(2)}, u32[]{:S(2)}) %collective-permute-start.4) | collective-permute-done | bytes 32800 | tf_op jit(solution)/shard_map/ppermute | solution.py:51
  126.3 0.0 collective-permute-done.5
  126.3 2.9 %all-to-all-done.5 = f32[8,16,512]{2,1,0:T(8,128)S(1)} async-done(((f32[8,16,512]{2,1,0:T(8,128)}), f32[8,16,512]{2,1,0:T(8,128)S(1)}, u32[]{:S(2)}, u32[]{:S(2)}) %all-to-all-start.5) | async-done | bytes 262176 | tf_op jit(solution)/shard_map/all_to_all | solution.py:15
  129.3 0.9 tile.21
  130.1 14.9 %all-to-all-start.6 = ((f32[8,32,512]{2,1,0:T(8,128)}), f32[8,32,512]{2,1,0:T(8,128)S(1)}, u32[]{:S(2)}, u32[]{:S(2)}) async-start(f32[8,32,512]{2,1,0:T(8,128)} %tile.21), calls=%async_computation.6 | async-start | bytes 1048576 | tf_op jit(solution)/shard_map/all_to_all | solution.py:15
  145.0 1.9 %collective-permute-start.3 = (f32[128,512]{1,0:T(8,128)S(1)}, f32[128,512]{1,0:T(8,128)S(1)}, u32[]{:S(2)}, u32[]{:S(2)}) collective-permute-start(f32[128,512]{1,0:T(8,128)S(1)} %bitcast.22), channel_id=1, source_target_pairs={{0,1},{1,0},{2,3},{3,2},{4,5},{5,4},{6,7},{7,6},{8,9},{9,8},{10,11... | collective-permute-start | bytes 786440 | tf_op jit(solution)/shard_map/ppermute | solution.py:53
  146.9 12.3 %all-to-all-done.6 = f32[8,32,512]{2,1,0:T(8,128)S(1)} async-done(((f32[8,32,512]{2,1,0:T(8,128)}), f32[8,32,512]{2,1,0:T(8,128)S(1)}, u32[]{:S(2)}, u32[]{:S(2)}) %all-to-all-start.6) | async-done | bytes 524320 | tf_op jit(solution)/shard_map/all_to_all | solution.py:15
  159.3 1.1 tile.23
  160.4 7.8 %all-to-all-start.7 = ((f32[2,256,512]{2,1,0:T(8,128)}), f32[2,256,512]{2,1,0:T(8,128)S(1)}, u32[]{:S(2)}, u32[]{:S(2)}) async-start(f32[2,256,512]{2,1,0:T(8,128)} %tile.23), calls=%async_computation.7 | async-start | bytes 2097152 | tf_op jit(solution)/shard_map/all_to_all | solution.py:15
  168.1 0.0 collective-permute-done.3
  168.1 1.7 %all-to-all-done.7 = f32[2,256,512]{2,1,0:T(8,128)S(1)} async-done(((f32[2,256,512]{2,1,0:T(8,128)}), f32[2,256,512]{2,1,0:T(8,128)S(1)}, u32[]{:S(2)}, u32[]{:S(2)}) %all-to-all-start.7) | async-done | bytes 1048608 | tf_op jit(solution)/shard_map/all_to_all | solution.py:15
  169.9 1.4 convolution_divide_fusion
  (4 shorter events, 0.1 us)
Async XLA Ops:
  0.0 1.0 copy-start
  29.1 14.1 %all-to-all-start.1 = ((f32[8,16,512]{2,1,0:T(8,128)}), f32[8,16,512]{2,1,0:T(8,128)S(1)}, u32[]{:S(2)}, u32[]{:S(2)}) async-start(f32[8,16,512]{2,1,0:T(8,128)} %tile.16), calls=%async_computation.1 | async-start | bytes 524288 | tf_op jit(solution)/shard_map/all_to_all | solution.py:15
  33.9 5.1 %collective-permute-start.1 = (f32[16,512]{1,0:T(8,128)S(1)}, f32[16,512]{1,0:T(8,128)S(1)}, u32[]{:S(2)}, u32[]{:S(2)}) collective-permute-start(f32[16,512]{1,0:T(8,128)S(1)} %reduce_sum.18), channel_id=1, source_target_pairs={{0,32},{1,288},{2,0},{3,256},{4,96},{5,352},{6,64},{7,320},{8,160}... | collective-permute-start | bytes 98312 | tf_op jit(solution)/shard_map/ppermute | solution.py:51
  36.1 2.9 %collective-permute-start.2 = (f32[16,512]{1,0:T(8,128)S(1)}, f32[16,512]{1,0:T(8,128)S(1)}, u32[]{:S(2)}, u32[]{:S(2)}) collective-permute-start(f32[16,512]{1,0:T(8,128)S(1)} %reduce_sum.18), channel_id=1, source_target_pairs={{0,0},{1,256},{2,32},{3,288},{4,64},{5,320},{6,96},{7,352},{8,128}... | collective-permute-start | bytes 98312 | tf_op jit(solution)/shard_map/ppermute | solution.py:50
  44.1 33.1 %all-to-all-start.2 = ((f32[8,32,512]{2,1,0:T(8,128)}), f32[8,32,512]{2,1,0:T(8,128)S(1)}, u32[]{:S(2)}, u32[]{:S(2)}) async-start(f32[8,32,512]{2,1,0:T(8,128)} %tile.17), calls=%async_computation.2 | async-start | bytes 1048576 | tf_op jit(solution)/shard_map/all_to_all | solution.py:15
  62.3 23.3 %collective-permute-start = (f32[128,512]{1,0:T(8,128)S(1)}, f32[128,512]{1,0:T(8,128)S(1)}, u32[]{:S(2)}, u32[]{:S(2)}) collective-permute-start(f32[128,512]{1,0:T(8,128)S(1)} %bitcast.20), channel_id=1, source_target_pairs={{0,1},{1,0},{2,3},{3,2},{4,5},{5,4},{6,7},{7,6},{8,9},{9,8},{10,11... | collective-permute-start | bytes 786440 | tf_op jit(solution)/shard_map/ppermute | solution.py:53
  78.3 9.1 %copy-start.2 = (f32[256,512]{1,0:T(8,128)S(1)}, f32[256,512]{1,0:T(8,128)}, u32[]{:S(2)}) copy-start(f32[256,512]{1,0:T(8,128)} %param.5) | copy-start | bytes 1572868
  78.3 9.1 %all-to-all-start.3 = ((f32[2,256,512]{2,1,0:T(8,128)}), f32[2,256,512]{2,1,0:T(8,128)S(1)}, u32[]{:S(2)}, u32[]{:S(2)}) async-start(f32[2,256,512]{2,1,0:T(8,128)} %tile.19), calls=%async_computation.3 | async-start | bytes 2097152 | tf_op jit(solution)/shard_map/all_to_all | solution.py:15
  87.4 1.2 copy-start.1
  113.7 15.5 %all-to-all-start.5 = ((f32[8,16,512]{2,1,0:T(8,128)}), f32[8,16,512]{2,1,0:T(8,128)S(1)}, u32[]{:S(2)}, u32[]{:S(2)}) async-start(f32[8,16,512]{2,1,0:T(8,128)} %tile.20), calls=%async_computation.5 | async-start | bytes 524288 | tf_op jit(solution)/shard_map/all_to_all | solution.py:15
  119.3 7.0 %collective-permute-start.4 = (f32[16,512]{1,0:T(8,128)S(1)}, f32[16,512]{1,0:T(8,128)S(1)}, u32[]{:S(2)}, u32[]{:S(2)}) collective-permute-start(f32[16,512]{1,0:T(8,128)S(1)} %reduce_sum.19), channel_id=1, source_target_pairs={{0,32},{1,288},{2,0},{3,256},{4,96},{5,352},{6,64},{7,320},{8,160}... | collective-permute-start | bytes 98312 | tf_op jit(solution)/shard_map/ppermute | solution.py:51
  121.7 4.6 %collective-permute-start.5 = (f32[16,512]{1,0:T(8,128)S(1)}, f32[16,512]{1,0:T(8,128)S(1)}, u32[]{:S(2)}, u32[]{:S(2)}) collective-permute-start(f32[16,512]{1,0:T(8,128)S(1)} %reduce_sum.19), channel_id=1, source_target_pairs={{0,0},{1,256},{2,32},{3,288},{4,64},{5,320},{6,96},{7,352},{8,128}... | collective-permute-start | bytes 98312 | tf_op jit(solution)/shard_map/ppermute | solution.py:50
  130.1 29.2 %all-to-all-start.6 = ((f32[8,32,512]{2,1,0:T(8,128)}), f32[8,32,512]{2,1,0:T(8,128)S(1)}, u32[]{:S(2)}, u32[]{:S(2)}) async-start(f32[8,32,512]{2,1,0:T(8,128)} %tile.21), calls=%async_computation.6 | async-start | bytes 1048576 | tf_op jit(solution)/shard_map/all_to_all | solution.py:15
  145.0 23.1 %collective-permute-start.3 = (f32[128,512]{1,0:T(8,128)S(1)}, f32[128,512]{1,0:T(8,128)S(1)}, u32[]{:S(2)}, u32[]{:S(2)}) collective-permute-start(f32[128,512]{1,0:T(8,128)S(1)} %bitcast.22), channel_id=1, source_target_pairs={{0,1},{1,0},{2,3},{3,2},{4,5},{5,4},{6,7},{7,6},{8,9},{9,8},{10,11... | collective-permute-start | bytes 786440 | tf_op jit(solution)/shard_map/ppermute | solution.py:53
  160.4 9.5 %all-to-all-start.7 = ((f32[2,256,512]{2,1,0:T(8,128)}), f32[2,256,512]{2,1,0:T(8,128)S(1)}, u32[]{:S(2)}, u32[]{:S(2)}) async-start(f32[2,256,512]{2,1,0:T(8,128)} %tile.23), calls=%async_computation.7 | async-start | bytes 2097152 | tf_op jit(solution)/shard_map/all_to_all | solution.py:15

commit v3 on v2

--- a/solution.py
+++ b/solution.py
@@ -30,30 +30,30 @@
     mine = lax.dynamic_slice_in_dim(factor, here_row % CORES * rows, rows, 0)
     mine = jnp.where(here_row // CORES == here_col, mine, 0.0)
     along_y = [[y * PAIR + u for y in range(line)] for u in range(PAIR)]
-    along_z = [[z * PAIR * CORES + q for z in range(line)] for q in range(PAIR * CORES)]
-    team = [[k * CORES + e for e in range(CORES)] for k in range(nrow // CORES)]
     across = [(c, c ^ 1) for c in range(ncol)]
-    turns = [[], []]
-    for r in range(nrow):
-        for c in range(ncol):
-            j = c % PAIR * line + c // PAIR
-            for t in range(PAIR):
-                to = (j // PAIR * PAIR + (j % PAIR ^ t)) * CORES + r % CORES
-                turns[t].append((r * ncol + c, to * ncol + r // CORES))
+    partner = [(r, r ^ 1) for r in range(nrow)]
+    turn = []
+    along_zv = [[] for _ in range(CORES)]
+    for u in range(PAIR):
+        for y in range(line):
+            place = (y + line // 2) % line * PAIR + u
+            for e in range(CORES):
+                along_zv[e].append(place * CORES + e)
+            for r in range(nrow):
+                turn.append((r * ncol + y * PAIR + u, (place * CORES + r % CORES) * ncol + r // CORES))
     odd_u = here_col % PAIR == 1
-    odd_v = here_row // CORES % PAIR == 1
+    odd_e = here_row % CORES == 1
     amp = amplitudes
-    for step in range(ITERS):
+    for _ in range(ITERS):
         part = jnp.dot(amp, factor, precision=PRECISION) * scale + mine
         terms = spread(part, "col", [sum(along_y, [])])
         piece = terms.reshape(ncol, rows // ncol, depth).sum(0)
-        near = lax.ppermute(piece, ("row", "col"), turns[0])
-        far = lax.ppermute(piece, ("row", "col"), turns[1])
+        turned = lax.ppermute(piece, ("row", "col"), turn)
         row_half = spread(jnp.tile(piece, (line, 1)), "col", along_y)
         row_rest = lax.ppermute(row_half, "col", across)
-        two = ordered(near, far, odd_v)
-        col_half = spread(jnp.tile(two, (line, 1)), "row", along_z)
-        z_cols = spread(jnp.tile(col_half, (CORES, 1)), "row", team)
+        col_half = spread(jnp.tile(turned, (ncol, 1)), "row", along_zv)
+        col_rest = lax.ppermute(col_half, "row", partner)
+        z_cols = ordered(col_half, col_rest, odd_e)
         z_rows = ordered(row_half, row_rest, odd_u)
         full = lax.dot_general(z_rows, z_cols, (((1,), (1,)), ((), ())), precision=PRECISION)
         amp = full / denominators

time: 172 us -> 162 us (0.942)
  the two profiles are of different devices: /device:TPU:1 before, /device:TPU:6 now
where the time goes in v3:
time: 162 us; the launch traced here: 161 us
  blocking collectives  77.4 us (48%)
  starting transfers between devices  39.6 us (24%)
  waiting for transfers between devices  36.8 us (23%)
  matrix products  4.78 us (3%)
  local copies, waits for them, and re-layouts  2.61 us (2%)
    all_to_all x4, blocking collectives, spread(): lax.all_to_all(block, axis, split_axis=0, concat_axis=0, axis_index_group...  77.4 us
    all_to_all x2, waiting for transfers between devices, spread(): lax.all_to_all(block, axis, split_axis=0, concat_axis=0, axis_index_group...  17.3 us
    ppermute x2, starting transfers between devices, local(): turned = lax.ppermute(piece, ('row', 'col'), turn)  15.6 us
    all_to_all x2, starting transfers between devices, spread(): lax.all_to_all(block, axis, split_axis=0, concat_axis=0, axis_index_group...  13.3 us
    ppermute x2, waiting for transfers between devices, local(): row_rest = lax.ppermute(row_half, 'col', across)  12.6 us
    ppermute x2, waiting for transfers between devices, local(): turned = lax.ppermute(piece, ('row', 'col'), turn)  6.87 us
    ppermute x2, starting transfers between devices, local(): row_rest = lax.ppermute(row_half, 'col', across)  6.84 us
    ppermute x2, starting transfers between devices, local(): col_rest = lax.ppermute(col_half, 'row', partner)  3.82 us
  transfers between devices with their start and end apart: 8, of which 6 were waited for; matrix products, arithmetic and copies ran while one was open for 0% of the time, Pallas kernels for 0%

profile of v3, /device:TPU:6, one launch (start us, length us, event | category | flops | bytes accessed | tf_op | source)
XLA Modules:
  0.0 161.4 jit_solution(7533884492596118268)
XLA Ops:
  0.0 0.0 copy-start
  0.0 1.0 copy-done
  1.0 2.1 %fusion = f32[256,512]{1,0:T(8,128)S(1)} fusion(f32[256,512]{1,0:T(8,128)S(1)} %copy-done, f32[512,512]{1,0:T(8,128)} %param.4, s32[]{:T(128)S(6)} %select_n.57, pred[]{:T(512)S(6)} %eq.14), kind=kOutput, calls=%fused_computation.4 | convolution fusion | flops 403046400 | bytes 2621445 | tf_op jit(solution)/shard_map/dot_general | solution.py:48
  3.1 24.3 %all_to_all.54 = f32[16,16,512]{2,1,0:T(8,128)S(1)} all-to-all(f32[16,16,512]{2,1,0:T(8,128)S(1)} %bitcast.11), channel_id=1, replica_groups={{0,2,4,6,8,10,12,14,1,3,5,7,9,11,13,15},{16,18,20,22,24,26,28,30,17,19,..., dimensions={0} | all-to-all | bytes 1048576 | tf_op jit(solution)/shard_map/all_to_all | solution.py:15
  27.4 10.9 %collective-permute-start.1 = (f32[16,512]{1,0:T(8,128)S(1)}, f32[16,512]{1,0:T(8,128)S(1)}, u32[]{:S(2)}, u32[]{:S(2)}) collective-permute-start(f32[16,512]{1,0:T(8,128)S(1)} %reduce_sum.18), channel_id=1, source_target_pairs={{0,256},{16,272},{32,257},{48,273},{64,258},{80,274},{96,259},{112... | collective-permute-start | bytes 98312 | tf_op jit(solution)/shard_map/ppermute | solution.py:51
  38.4 1.6 collective-permute-done.1
  40.0 20.1 %all_to_all.55 = f32[16,16,512]{2,1,0:T(8,128)S(1)} all-to-all(f32[16,16,512]{2,1,0:T(8,128)S(1)} %tile.9), channel_id=1, replica_groups={{256,320,384,448,0,64,128,192,288,352,416,480,32,96,160,224},{272,336,4..., dimensions={0} | all-to-all | bytes 1048576 | tf_op jit(solution)/shard_map/all_to_all | solution.py:15
  60.1 0.0 copy-start.2
  60.1 0.7 tile.8
  60.8 7.6 %all-to-all-start.1 = ((f32[8,16,512]{2,1,0:T(8,128)}), f32[8,16,512]{2,1,0:T(8,128)S(1)}, u32[]{:S(2)}, u32[]{:S(2)}) async-start(f32[8,16,512]{2,1,0:T(8,128)} %tile.8), calls=%async_computation.1 | async-start | bytes 524288 | tf_op jit(solution)/shard_map/all_to_all | solution.py:15
  68.4 1.9 %collective-permute-start.2 = (f32[256,512]{1,0:T(8,128)S(1)}, f32[256,512]{1,0:T(8,128)S(1)}, u32[]{:S(2)}, u32[]{:S(2)}) collective-permute-start(f32[256,512]{1,0:T(8,128)S(1)} %bitcast.12), channel_id=1, source_target_pairs={{0,16},{16,0},{32,48},{48,32},{64,80},{80,64},{96,112},{112,96},{1... | collective-permute-start | bytes 1572872 | tf_op jit(solution)/shard_map/ppermute | solution.py:55
  70.3 8.7 %all-to-all-done.1 = f32[8,16,512]{2,1,0:T(8,128)S(1)} async-done(((f32[8,16,512]{2,1,0:T(8,128)}), f32[8,16,512]{2,1,0:T(8,128)S(1)}, u32[]{:S(2)}, u32[]{:S(2)}) %all-to-all-start.1) | async-done | bytes 262176 | tf_op jit(solution)/shard_map/all_to_all | solution.py:15
  79.0 4.2 %collective-permute-start = (f32[128,512]{1,0:T(8,128)S(1)}, f32[128,512]{1,0:T(8,128)S(1)}, u32[]{:S(2)}, u32[]{:S(2)}) collective-permute-start(f32[128,512]{1,0:T(8,128)S(1)} %bitcast.16), channel_id=1, source_target_pairs={{0,1},{1,0},{2,3},{3,2},{4,5},{5,4},{6,7},{7,6},{8,9},{9,8},{10,11... | collective-permute-start | bytes 786440 | tf_op jit(solution)/shard_map/ppermute | solution.py:53
  83.3 0.0 copy-start.1
  83.3 5.5 %collective-permute-done = f32[128,512]{1,0:T(8,128)S(1)} collective-permute-done((f32[128,512]{1,0:T(8,128)S(1)}, f32[128,512]{1,0:T(8,128)S(1)}, u32[]{:S(2)}, u32[]{:S(2)}) %collective-permute-start) | collective-permute-done | bytes 262176 | tf_op jit(solution)/shard_map/ppermute | solution.py:53
  88.8 0.0 collective-permute-done.2
  88.8 0.0 copy-done.2
  88.8 0.6 convolution_divide_fusion.1
  89.4 0.0 copy-done.1
  89.4 0.7 fusion.1
  90.1 16.2 %all_to_all.56 = f32[16,16,512]{2,1,0:T(8,128)S(1)} all-to-all(f32[16,16,512]{2,1,0:T(8,128)S(1)} %bitcast.10), channel_id=1, replica_groups={{0,2,4,6,8,10,12,14,1,3,5,7,9,11,13,15},{16,18,20,22,24,26,28,30,17,19,..., dimensions={0} | all-to-all | bytes 1048576 | tf_op jit(solution)/shard_map/all_to_all | solution.py:15
  106.4 4.7 %collective-permute-start.4 = (f32[16,512]{1,0:T(8,128)S(1)}, f32[16,512]{1,0:T(8,128)S(1)}, u32[]{:S(2)}, u32[]{:S(2)}) collective-permute-start(f32[16,512]{1,0:T(8,128)S(1)} %reduce_sum.19), channel_id=1, source_target_pairs={{0,256},{16,272},{32,257},{48,273},{64,258},{80,274},{96,259},{112... | collective-permute-start | bytes 98312 | tf_op jit(solution)/shard_map/ppermute | solution.py:51
  111.1 5.3 %collective-permute-done.4 = f32[16,512]{1,0:T(8,128)S(1)} collective-permute-done((f32[16,512]{1,0:T(8,128)S(1)}, f32[16,512]{1,0:T(8,128)S(1)}, u32[]{:S(2)}, u32[]{:S(2)}) %collective-permute-start.4) | collective-permute-done | bytes 32800 | tf_op jit(solution)/shard_map/ppermute | solution.py:51
  116.4 16.8 %all_to_all.57 = f32[16,16,512]{2,1,0:T(8,128)S(1)} all-to-all(f32[16,16,512]{2,1,0:T(8,128)S(1)} %tile.11), channel_id=1, replica_groups={{256,320,384,448,0,64,128,192,288,352,416,480,32,96,160,224},{272,336,4..., dimensions={0} | all-to-all | bytes 1048576 | tf_op jit(solution)/shard_map/all_to_all | solution.py:15
  133.2 0.7 tile.10
  133.9 5.8 %all-to-all-start.4 = ((f32[8,16,512]{2,1,0:T(8,128)}), f32[8,16,512]{2,1,0:T(8,128)S(1)}, u32[]{:S(2)}, u32[]{:S(2)}) async-start(f32[8,16,512]{2,1,0:T(8,128)} %tile.10), calls=%async_computation.4 | async-start | bytes 524288 | tf_op jit(solution)/shard_map/all_to_all | solution.py:15
  139.7 1.9 %collective-permute-start.5 = (f32[256,512]{1,0:T(8,128)S(1)}, f32[256,512]{1,0:T(8,128)S(1)}, u32[]{:S(2)}, u32[]{:S(2)}) collective-permute-start(f32[256,512]{1,0:T(8,128)S(1)} %bitcast.14), channel_id=1, source_target_pairs={{0,16},{16,0},{32,48},{48,32},{64,80},{80,64},{96,112},{112,96},{1... | collective-permute-start | bytes 1572872 | tf_op jit(solution)/shard_map/ppermute | solution.py:55
  141.6 8.6 %all-to-all-done.4 = f32[8,16,512]{2,1,0:T(8,128)S(1)} async-done(((f32[8,16,512]{2,1,0:T(8,128)}), f32[8,16,512]{2,1,0:T(8,128)S(1)}, u32[]{:S(2)}, u32[]{:S(2)}) %all-to-all-start.4) | async-done | bytes 262176 | tf_op jit(solution)/shard_map/all_to_all | solution.py:15
  150.2 2.6 %collective-permute-start.3 = (f32[128,512]{1,0:T(8,128)S(1)}, f32[128,512]{1,0:T(8,128)S(1)}, u32[]{:S(2)}, u32[]{:S(2)}) collective-permute-start(f32[128,512]{1,0:T(8,128)S(1)} %bitcast.18), channel_id=1, source_target_pairs={{0,1},{1,0},{2,3},{3,2},{4,5},{5,4},{6,7},{7,6},{8,9},{9,8},{10,11... | collective-permute-start | bytes 786440 | tf_op jit(solution)/shard_map/ppermute | solution.py:53
  152.8 7.1 %collective-permute-done.3 = f32[128,512]{1,0:T(8,128)S(1)} collective-permute-done((f32[128,512]{1,0:T(8,128)S(1)}, f32[128,512]{1,0:T(8,128)S(1)}, u32[]{:S(2)}, u32[]{:S(2)}) %collective-permute-start.3) | collective-permute-done | bytes 262176 | tf_op jit(solution)/shard_map/ppermute | solution.py:53
  159.9 0.0 collective-permute-done.5
  159.9 1.4 convolution_divide_fusion
  (4 shorter events, 0.2 us)
Async XLA Ops:
  0.0 1.0 copy-start
  27.4 12.5 %collective-permute-start.1 = (f32[16,512]{1,0:T(8,128)S(1)}, f32[16,512]{1,0:T(8,128)S(1)}, u32[]{:S(2)}, u32[]{:S(2)}) collective-permute-start(f32[16,512]{1,0:T(8,128)S(1)} %reduce_sum.18), channel_id=1, source_target_pairs={{0,256},{16,272},{32,257},{48,273},{64,258},{80,274},{96,259},{112... | collective-permute-start | bytes 98312 | tf_op jit(solution)/shard_map/ppermute | solution.py:51
  60.1 28.7 %copy-start.2 = (f32[256,512]{1,0:T(8,128)S(1)}, f32[256,512]{1,0:T(8,128)}, u32[]{:S(2)}) copy-start(f32[256,512]{1,0:T(8,128)} %param.5) | copy-start | bytes 1572868
  60.8 18.2 %all-to-all-start.1 = ((f32[8,16,512]{2,1,0:T(8,128)}), f32[8,16,512]{2,1,0:T(8,128)S(1)}, u32[]{:S(2)}, u32[]{:S(2)}) async-start(f32[8,16,512]{2,1,0:T(8,128)} %tile.8), calls=%async_computation.1 | async-start | bytes 524288 | tf_op jit(solution)/shard_map/all_to_all | solution.py:15
  68.4 20.4 %collective-permute-start.2 = (f32[256,512]{1,0:T(8,128)S(1)}, f32[256,512]{1,0:T(8,128)S(1)}, u32[]{:S(2)}, u32[]{:S(2)}) collective-permute-start(f32[256,512]{1,0:T(8,128)S(1)} %bitcast.12), channel_id=1, source_target_pairs={{0,16},{16,0},{32,48},{48,32},{64,80},{80,64},{96,112},{112,96},{1... | collective-permute-start | bytes 1572872 | tf_op jit(solution)/shard_map/ppermute | solution.py:55
  79.0 9.8 %collective-permute-start = (f32[128,512]{1,0:T(8,128)S(1)}, f32[128,512]{1,0:T(8,128)S(1)}, u32[]{:S(2)}, u32[]{:S(2)}) collective-permute-start(f32[128,512]{1,0:T(8,128)S(1)} %bitcast.16), channel_id=1, source_target_pairs={{0,1},{1,0},{2,3},{3,2},{4,5},{5,4},{6,7},{7,6},{8,9},{9,8},{10,11... | collective-permute-start | bytes 786440 | tf_op jit(solution)/shard_map/ppermute | solution.py:53
  83.3 6.1 %copy-start.1 = (f32[512,512]{1,0:T(8,128)S(1)}, f32[512,512]{1,0:T(8,128)}, u32[]{:S(2)}) copy-start(f32[512,512]{1,0:T(8,128)} %param.4) | copy-start | bytes 3145732
  106.4 10.0 %collective-permute-start.4 = (f32[16,512]{1,0:T(8,128)S(1)}, f32[16,512]{1,0:T(8,128)S(1)}, u32[]{:S(2)}, u32[]{:S(2)}) collective-permute-start(f32[16,512]{1,0:T(8,128)S(1)} %reduce_sum.19), channel_id=1, source_target_pairs={{0,256},{16,272},{32,257},{48,273},{64,258},{80,274},{96,259},{112... | collective-permute-start | bytes 98312 | tf_op jit(solution)/shard_map/ppermute | solution.py:51
  133.9 16.2 %all-to-all-start.4 = ((f32[8,16,512]{2,1,0:T(8,128)}), f32[8,16,512]{2,1,0:T(8,128)S(1)}, u32[]{:S(2)}, u32[]{:S(2)}) async-start(f32[8,16,512]{2,1,0:T(8,128)} %tile.10), calls=%async_computation.4 | async-start | bytes 524288 | tf_op jit(solution)/shard_map/all_to_all | solution.py:15
  139.7 20.2 %collective-permute-start.5 = (f32[256,512]{1,0:T(8,128)S(1)}, f32[256,512]{1,0:T(8,128)S(1)}, u32[]{:S(2)}, u32[]{:S(2)}) collective-permute-start(f32[256,512]{1,0:T(8,128)S(1)} %bitcast.14), channel_id=1, source_target_pairs={{0,16},{16,0},{32,48},{48,32},{64,80},{80,64},{96,112},{112,96},{1... | collective-permute-start | bytes 1572872 | tf_op jit(solution)/shard_map/ppermute | solution.py:55
  150.2 9.8 %collective-permute-start.3 = (f32[128,512]{1,0:T(8,128)S(1)}, f32[128,512]{1,0:T(8,128)S(1)}, u32[]{:S(2)}, u32[]{:S(2)}) collective-permute-start(f32[128,512]{1,0:T(8,128)S(1)} %bitcast.18), channel_id=1, source_target_pairs={{0,1},{1,0},{2,3},{3,2},{4,5},{5,4},{6,7},{7,6},{8,9},{9,8},{10,11... | collective-permute-start | bytes 786440 | tf_op jit(solution)/shard_map/ppermute | solution.py:53

commit v4 on v3

--- a/solution.py
+++ b/solution.py
@@ -48,13 +48,14 @@
         part = jnp.dot(amp, factor, precision=PRECISION) * scale + mine
         terms = spread(part, "col", [sum(along_y, [])])
         piece = terms.reshape(ncol, rows // ncol, depth).sum(0)
+        row_half = spread(jnp.tile(piece, (line, 1)), "col", along_y)
         turned = lax.ppermute(piece, ("row", "col"), turn)
-        row_half = spread(jnp.tile(piece, (line, 1)), "col", along_y)
+        copies = jnp.tile(turned, (ncol, 1))
+        col_half = spread(copies, "row", along_zv)
         row_rest = lax.ppermute(row_half, "col", across)
-        col_half = spread(jnp.tile(turned, (ncol, 1)), "row", along_zv)
+        z_rows = lax.optimization_barrier(ordered(row_half, row_rest, odd_u))
         col_rest = lax.ppermute(col_half, "row", partner)
         z_cols = ordered(col_half, col_rest, odd_e)
-        z_rows = ordered(row_half, row_rest, odd_u)
         full = lax.dot_general(z_rows, z_cols, (((1,), (1,)), ((), ())), precision=PRECISION)
         amp = full / denominators
     return amp

time: 162 us -> 163 us (level)
  no operation moved by 1% of the time
where the time goes in v4:
time: 163 us; the launch traced here: 162 us
  blocking collectives  77.4 us (47%)
  starting transfers between devices  39.6 us (24%)
  waiting for transfers between devices  36.8 us (23%)
  matrix products  4.71 us (3%)
  local copies, waits for them, and re-layouts  3.18 us (2%)
    all_to_all x4, blocking collectives, spread(): lax.all_to_all(block, axis, split_axis=0, concat_axis=0, axis_index_group...  77.4 us
    all_to_all x2, waiting for transfers between devices, spread(): lax.all_to_all(block, axis, split_axis=0, concat_axis=0, axis_index_group...  17.3 us
    ppermute x2, starting transfers between devices, local(): turned = lax.ppermute(piece, ('row', 'col'), turn)  15.6 us
    all_to_all x2, starting transfers between devices, spread(): lax.all_to_all(block, axis, split_axis=0, concat_axis=0, axis_index_group...  13.3 us
    ppermute x2, waiting for transfers between devices, local(): row_rest = lax.ppermute(row_half, 'col', across)  12.6 us
    ppermute x2, waiting for transfers between devices, local(): turned = lax.ppermute(piece, ('row', 'col'), turn)  6.87 us
    ppermute x2, starting transfers between devices, local(): row_rest = lax.ppermute(row_half, 'col', across)  6.84 us
    ppermute x2, starting transfers between devices, local(): col_rest = lax.ppermute(col_half, 'row', partner)  3.82 us
  transfers between devices with their start and end apart: 8, of which 6 were waited for; matrix products, arithmetic and copies ran while one was open for 0% of the time, Pallas kernels for 0%

profile of v4, /device:TPU:6, one launch (start us, length us, event | category | flops | bytes accessed | tf_op | source)
XLA Modules:
  0.0 162.0 jit_solution(608531970943650136)
XLA Ops:
  0.0 0.0 copy-start
  0.0 1.0 copy-done
  1.0 2.1 %fusion = f32[256,512]{1,0:T(8,128)S(1)} fusion(f32[256,512]{1,0:T(8,128)S(1)} %copy-done, f32[512,512]{1,0:T(8,128)} %param.4, s32[]{:T(128)S(6)} %select_n.57, pred[]{:T(512)S(6)} %eq.14), kind=kOutput, calls=%fused_computation.4 | convolution fusion | flops 403046400 | bytes 2621445 | tf_op jit(solution)/shard_map/dot_general | solution.py:48
  3.1 24.3 %all_to_all.54 = f32[16,16,512]{2,1,0:T(8,128)S(1)} all-to-all(f32[16,16,512]{2,1,0:T(8,128)S(1)} %bitcast.13), channel_id=1, replica_groups={{0,2,4,6,8,10,12,14,1,3,5,7,9,11,13,15},{16,18,20,22,24,26,28,30,17,19,..., dimensions={0} | all-to-all | bytes 1048576 | tf_op jit(solution)/shard_map/all_to_all | solution.py:15
  27.4 10.9 %collective-permute-start.1 = (f32[16,512]{1,0:T(8,128)S(1)}, f32[16,512]{1,0:T(8,128)S(1)}, u32[]{:S(2)}, u32[]{:S(2)}) collective-permute-start(f32[16,512]{1,0:T(8,128)S(1)} %reduce_sum.18), channel_id=1, source_target_pairs={{0,256},{16,272},{32,257},{48,273},{64,258},{80,274},{96,259},{112... | collective-permute-start | bytes 98312 | tf_op jit(solution)/shard_map/ppermute | solution.py:52
  38.4 1.6 collective-permute-done.1
  40.0 20.1 %all_to_all.55 = f32[16,16,512]{2,1,0:T(8,128)S(1)} all-to-all(f32[16,16,512]{2,1,0:T(8,128)S(1)} %tile.9), channel_id=1, replica_groups={{256,320,384,448,0,64,128,192,288,352,416,480,32,96,160,224},{272,336,4..., dimensions={0} | all-to-all | bytes 1048576 | tf_op jit(solution)/shard_map/all_to_all | solution.py:15
  60.1 0.7 tile.8
  60.8 7.6 %all-to-all-start.1 = ((f32[8,16,512]{2,1,0:T(8,128)}), f32[8,16,512]{2,1,0:T(8,128)S(1)}, u32[]{:S(2)}, u32[]{:S(2)}) async-start(f32[8,16,512]{2,1,0:T(8,128)} %tile.8), calls=%async_computation.1 | async-start | bytes 524288 | tf_op jit(solution)/shard_map/all_to_all | solution.py:15
  68.4 1.9 %collective-permute-start.2 = (f32[256,512]{1,0:T(8,128)S(1)}, f32[256,512]{1,0:T(8,128)S(1)}, u32[]{:S(2)}, u32[]{:S(2)}) collective-permute-start(f32[256,512]{1,0:T(8,128)S(1)} %bitcast.18), channel_id=1, source_target_pairs={{0,16},{16,0},{32,48},{48,32},{64,80},{80,64},{96,112},{112,96},{1... | collective-permute-start | bytes 1572872 | tf_op jit(solution)/shard_map/ppermute | solution.py:57
  70.3 8.7 %all-to-all-done.1 = f32[8,16,512]{2,1,0:T(8,128)S(1)} async-done(((f32[8,16,512]{2,1,0:T(8,128)}), f32[8,16,512]{2,1,0:T(8,128)S(1)}, u32[]{:S(2)}, u32[]{:S(2)}) %all-to-all-start.1) | async-done | bytes 262176 | tf_op jit(solution)/shard_map/all_to_all | solution.py:15
  79.0 4.2 %collective-permute-start = (f32[128,512]{1,0:T(8,128)S(1)}, f32[128,512]{1,0:T(8,128)S(1)}, u32[]{:S(2)}, u32[]{:S(2)}) collective-permute-start(f32[128,512]{1,0:T(8,128)S(1)} %bitcast.14), channel_id=1, source_target_pairs={{0,1},{1,0},{2,3},{3,2},{4,5},{5,4},{6,7},{7,6},{8,9},{9,8},{10,11... | collective-permute-start | bytes 786440 | tf_op jit(solution)/shard_map/ppermute | solution.py:55
  83.3 0.0 copy-start.2
  83.3 5.5 %collective-permute-done = f32[128,512]{1,0:T(8,128)S(1)} collective-permute-done((f32[128,512]{1,0:T(8,128)S(1)}, f32[128,512]{1,0:T(8,128)S(1)}, u32[]{:S(2)}, u32[]{:S(2)}) %collective-permute-start) | collective-permute-done | bytes 262176 | tf_op jit(solution)/shard_map/ppermute | solution.py:55
  88.8 0.0 copy-start.1
  88.8 0.0 collective-permute-done.2
  88.9 0.0 copy-done.2
  88.9 0.6 convolution_divide_fusion.1
  89.5 0.6 copy-done.1
  90.1 0.6 fusion.1
  90.7 16.3 %all_to_all.56 = f32[16,16,512]{2,1,0:T(8,128)S(1)} all-to-all(f32[16,16,512]{2,1,0:T(8,128)S(1)} %bitcast.12), channel_id=1, replica_groups={{0,2,4,6,8,10,12,14,1,3,5,7,9,11,13,15},{16,18,20,22,24,26,28,30,17,19,..., dimensions={0} | all-to-all | bytes 1048576 | tf_op jit(solution)/shard_map/all_to_all | solution.py:15
  107.0 4.7 %collective-permute-start.4 = (f32[16,512]{1,0:T(8,128)S(1)}, f32[16,512]{1,0:T(8,128)S(1)}, u32[]{:S(2)}, u32[]{:S(2)}) collective-permute-start(f32[16,512]{1,0:T(8,128)S(1)} %reduce_sum.19), channel_id=1, source_target_pairs={{0,256},{16,272},{32,257},{48,273},{64,258},{80,274},{96,259},{112... | collective-permute-start | bytes 98312 | tf_op jit(solution)/shard_map/ppermute | solution.py:52
  111.7 5.3 %collective-permute-done.4 = f32[16,512]{1,0:T(8,128)S(1)} collective-permute-done((f32[16,512]{1,0:T(8,128)S(1)}, f32[16,512]{1,0:T(8,128)S(1)}, u32[]{:S(2)}, u32[]{:S(2)}) %collective-permute-start.4) | collective-permute-done | bytes 32800 | tf_op jit(solution)/shard_map/ppermute | solution.py:52
  117.0 16.8 %all_to_all.57 = f32[16,16,512]{2,1,0:T(8,128)S(1)} all-to-all(f32[16,16,512]{2,1,0:T(8,128)S(1)} %tile.11), channel_id=1, replica_groups={{256,320,384,448,0,64,128,192,288,352,416,480,32,96,160,224},{272,336,4..., dimensions={0} | all-to-all | bytes 1048576 | tf_op jit(solution)/shard_map/all_to_all | solution.py:15
  133.8 0.7 tile.10
  134.5 5.8 %all-to-all-start.4 = ((f32[8,16,512]{2,1,0:T(8,128)}), f32[8,16,512]{2,1,0:T(8,128)S(1)}, u32[]{:S(2)}, u32[]{:S(2)}) async-start(f32[8,16,512]{2,1,0:T(8,128)} %tile.10), calls=%async_computation.4 | async-start | bytes 524288 | tf_op jit(solution)/shard_map/all_to_all | solution.py:15
  140.3 1.9 %collective-permute-start.5 = (f32[256,512]{1,0:T(8,128)S(1)}, f32[256,512]{1,0:T(8,128)S(1)}, u32[]{:S(2)}, u32[]{:S(2)}) collective-permute-start(f32[256,512]{1,0:T(8,128)S(1)} %bitcast.20), channel_id=1, source_target_pairs={{0,16},{16,0},{32,48},{48,32},{64,80},{80,64},{96,112},{112,96},{1... | collective-permute-start | bytes 1572872 | tf_op jit(solution)/shard_map/ppermute | solution.py:57
  142.2 8.6 %all-to-all-done.4 = f32[8,16,512]{2,1,0:T(8,128)S(1)} async-done(((f32[8,16,512]{2,1,0:T(8,128)}), f32[8,16,512]{2,1,0:T(8,128)S(1)}, u32[]{:S(2)}, u32[]{:S(2)}) %all-to-all-start.4) | async-done | bytes 262176 | tf_op jit(solution)/shard_map/all_to_all | solution.py:15
  150.8 2.6 %collective-permute-start.3 = (f32[128,512]{1,0:T(8,128)S(1)}, f32[128,512]{1,0:T(8,128)S(1)}, u32[]{:S(2)}, u32[]{:S(2)}) collective-permute-start(f32[128,512]{1,0:T(8,128)S(1)} %bitcast.16), channel_id=1, source_target_pairs={{0,1},{1,0},{2,3},{3,2},{4,5},{5,4},{6,7},{7,6},{8,9},{9,8},{10,11... | collective-permute-start | bytes 786440 | tf_op jit(solution)/shard_map/ppermute | solution.py:55
  153.4 7.1 %collective-permute-done.3 = f32[128,512]{1,0:T(8,128)S(1)} collective-permute-done((f32[128,512]{1,0:T(8,128)S(1)}, f32[128,512]{1,0:T(8,128)S(1)}, u32[]{:S(2)}, u32[]{:S(2)}) %collective-permute-start.3) | collective-permute-done | bytes 262176 | tf_op jit(solution)/shard_map/ppermute | solution.py:55
  160.6 0.0 collective-permute-done.5
  160.6 1.4 convolution_divide_fusion
  (6 shorter events, 0.3 us)
Async XLA Ops:
  0.0 1.0 copy-start
  27.4 12.5 %collective-permute-start.1 = (f32[16,512]{1,0:T(8,128)S(1)}, f32[16,512]{1,0:T(8,128)S(1)}, u32[]{:S(2)}, u32[]{:S(2)}) collective-permute-start(f32[16,512]{1,0:T(8,128)S(1)} %reduce_sum.18), channel_id=1, source_target_pairs={{0,256},{16,272},{32,257},{48,273},{64,258},{80,274},{96,259},{112... | collective-permute-start | bytes 98312 | tf_op jit(solution)/shard_map/ppermute | solution.py:52
  60.8 18.2 %all-to-all-start.1 = ((f32[8,16,512]{2,1,0:T(8,128)}), f32[8,16,512]{2,1,0:T(8,128)S(1)}, u32[]{:S(2)}, u32[]{:S(2)}) async-start(f32[8,16,512]{2,1,0:T(8,128)} %tile.8), calls=%async_computation.1 | async-start | bytes 524288 | tf_op jit(solution)/shard_map/all_to_all | solution.py:15
  68.4 20.5 %collective-permute-start.2 = (f32[256,512]{1,0:T(8,128)S(1)}, f32[256,512]{1,0:T(8,128)S(1)}, u32[]{:S(2)}, u32[]{:S(2)}) collective-permute-start(f32[256,512]{1,0:T(8,128)S(1)} %bitcast.18), channel_id=1, source_target_pairs={{0,16},{16,0},{32,48},{48,32},{64,80},{80,64},{96,112},{112,96},{1... | collective-permute-start | bytes 1572872 | tf_op jit(solution)/shard_map/ppermute | solution.py:57
  79.0 9.8 %collective-permute-start = (f32[128,512]{1,0:T(8,128)S(1)}, f32[128,512]{1,0:T(8,128)S(1)}, u32[]{:S(2)}, u32[]{:S(2)}) collective-permute-start(f32[128,512]{1,0:T(8,128)S(1)} %bitcast.14), channel_id=1, source_target_pairs={{0,1},{1,0},{2,3},{3,2},{4,5},{5,4},{6,7},{7,6},{8,9},{9,8},{10,11... | collective-permute-start | bytes 786440 | tf_op jit(solution)/shard_map/ppermute | solution.py:55
  83.3 5.6 %copy-start.2 = (f32[256,512]{1,0:T(8,128)S(1)}, f32[256,512]{1,0:T(8,128)}, u32[]{:S(2)}) copy-start(f32[256,512]{1,0:T(8,128)} %param.5) | copy-start | bytes 1572868
  88.8 1.2 copy-start.1
  107.0 10.0 %collective-permute-start.4 = (f32[16,512]{1,0:T(8,128)S(1)}, f32[16,512]{1,0:T(8,128)S(1)}, u32[]{:S(2)}, u32[]{:S(2)}) collective-permute-start(f32[16,512]{1,0:T(8,128)S(1)} %reduce_sum.19), channel_id=1, source_target_pairs={{0,256},{16,272},{32,257},{48,273},{64,258},{80,274},{96,259},{112... | collective-permute-start | bytes 98312 | tf_op jit(solution)/shard_map/ppermute | solution.py:52
  134.5 16.2 %all-to-all-start.4 = ((f32[8,16,512]{2,1,0:T(8,128)}), f32[8,16,512]{2,1,0:T(8,128)S(1)}, u32[]{:S(2)}, u32[]{:S(2)}) async-start(f32[8,16,512]{2,1,0:T(8,128)} %tile.10), calls=%async_computation.4 | async-start | bytes 524288 | tf_op jit(solution)/shard_map/all_to_all | solution.py:15
  140.3 20.3 %collective-permute-start.5 = (f32[256,512]{1,0:T(8,128)S(1)}, f32[256,512]{1,0:T(8,128)S(1)}, u32[]{:S(2)}, u32[]{:S(2)}) collective-permute-start(f32[256,512]{1,0:T(8,128)S(1)} %bitcast.20), channel_id=1, source_target_pairs={{0,16},{16,0},{32,48},{48,32},{64,80},{80,64},{96,112},{112,96},{1... | collective-permute-start | bytes 1572872 | tf_op jit(solution)/shard_map/ppermute | solution.py:57
  150.8 9.8 %collective-permute-start.3 = (f32[128,512]{1,0:T(8,128)S(1)}, f32[128,512]{1,0:T(8,128)S(1)}, u32[]{:S(2)}, u32[]{:S(2)}) collective-permute-start(f32[128,512]{1,0:T(8,128)S(1)} %bitcast.16), channel_id=1, source_target_pairs={{0,1},{1,0},{2,3},{3,2},{4,5},{5,4},{6,7},{7,6},{8,9},{9,8},{10,11... | collective-permute-start | bytes 786440 | tf_op jit(solution)/shard_map/ppermute | solution.py:55

commit v5 on v4

--- a/solution.py
+++ b/solution.py
@@ -29,31 +29,25 @@
     scale = 1.0 / math.sqrt(rows * nrow)
     mine = lax.dynamic_slice_in_dim(factor, here_row % CORES * rows, rows, 0)
     mine = jnp.where(here_row // CORES == here_col, mine, 0.0)
-    along_y = [[y * PAIR + u for y in range(line)] for u in range(PAIR)]
-    across = [(c, c ^ 1) for c in range(ncol)]
     partner = [(r, r ^ 1) for r in range(nrow)]
     turn = []
     along_zv = [[] for _ in range(CORES)]
-    for u in range(PAIR):
-        for y in range(line):
-            place = (y + line // 2) % line * PAIR + u
-            for e in range(CORES):
-                along_zv[e].append(place * CORES + e)
-            for r in range(nrow):
-                turn.append((r * ncol + y * PAIR + u, (place * CORES + r % CORES) * ncol + r // CORES))
-    odd_u = here_col % PAIR == 1
+    for c in range(ncol):
+        place = (c // PAIR + line // 2) % line * PAIR + c % PAIR
+        for e in range(CORES):
+            along_zv[e].append(place * CORES + e)
+        for r in range(nrow):
+            turn.append((r * ncol + c, (place * CORES + r % CORES) * ncol + r // CORES))
     odd_e = here_row % CORES == 1
     amp = amplitudes
     for _ in range(ITERS):
         part = jnp.dot(amp, factor, precision=PRECISION) * scale + mine
-        terms = spread(part, "col", [sum(along_y, [])])
+        terms = spread(part, "col", None)
         piece = terms.reshape(ncol, rows // ncol, depth).sum(0)
-        row_half = spread(jnp.tile(piece, (line, 1)), "col", along_y)
+        z_rows = spread(jnp.tile(piece, (ncol, 1)), "col", None)
         turned = lax.ppermute(piece, ("row", "col"), turn)
         copies = jnp.tile(turned, (ncol, 1))
         col_half = spread(copies, "row", along_zv)
-        row_rest = lax.ppermute(row_half, "col", across)
-        z_rows = lax.optimization_barrier(ordered(row_half, row_rest, odd_u))
         col_rest = lax.ppermute(col_half, "row", partner)
         z_cols = ordered(col_half, col_rest, odd_e)
         full = lax.dot_general(z_rows, z_cols, (((1,), (1,)), ((), ())), precision=PRECISION)

time: 163 us -> 168 us (1.031)
  the two profiles are of different devices: /device:TPU:6 before, /device:TPU:1 now
where the time goes in v5:
time: 168 us; the launch traced here: 167 us
  blocking collectives  88.8 us (53%)
  starting transfers between devices  36.2 us (22%)
  waiting for transfers between devices  34.2 us (20%)
  matrix products  4.63 us (3%)
  local copies, waits for them, and re-layouts  3.44 us (2%)
    all_to_all x4, blocking collectives, spread(): lax.all_to_all(block, axis, split_axis=0, concat_axis=0, axis_index_group...  88.8 us
    all_to_all x2, waiting for transfers between devices, spread(): lax.all_to_all(block, axis, split_axis=0, concat_axis=0, axis_index_group...  26.5 us
    all_to_all x2, starting transfers between devices, spread(): lax.all_to_all(block, axis, split_axis=0, concat_axis=0, axis_index_group...  16.6 us
    ppermute x2, starting transfers between devices, local(): turned = lax.ppermute(piece, ('row', 'col'), turn)  12.6 us
    ppermute x2, waiting for transfers between devices, local(): turned = lax.ppermute(piece, ('row', 'col'), turn)  7.64 us
    ppermute x2, starting transfers between devices, local(): col_rest = lax.ppermute(col_half, 'row', partner)  6.99 us
  transfers between devices with their start and end apart: 6, of which 4 were waited for; matrix products, arithmetic and copies ran while one was open for 0% of the time, Pallas kernels for 0%

profile of v5, /device:TPU:1, one launch (start us, length us, event | category | flops | bytes accessed | tf_op | source)
XLA Modules:
  0.0 167.4 jit_solution(15805063472917309745)
XLA Ops:
  0.0 0.0 copy-start
  0.0 1.0 copy-done
  1.0 2.0 %fusion = f32[256,512]{1,0:T(8,128)S(1)} fusion(f32[256,512]{1,0:T(8,128)S(1)} %copy-done, f32[512,512]{1,0:T(8,128)} %param.4, s32[]{:T(128)S(6)} %select_n.39, pred[]{:T(512)S(6)} %eq.9), kind=kOutput, calls=%fused_computation.4 | convolution fusion | flops 403046400 | bytes 2621445 | tf_op jit(solution)/shard_map/dot_general | solution.py:44
  3.0 27.2 %all_to_all.54 = f32[16,16,512]{2,1,0:T(8,128)S(1)} all-to-all(f32[16,16,512]{2,1,0:T(8,128)S(1)} %bitcast.13), channel_id=1, replica_groups=mesh['row'=32,'col'=16] {'col'}, dimensions={0} | all-to-all | bytes 1048576 | tf_op jit(solution)/shard_map/all_to_all | solution.py:15
  30.3 10.6 %collective-permute-start = (f32[16,512]{1,0:T(8,128)S(1)}, f32[16,512]{1,0:T(8,128)S(1)}, u32[]{:S(2)}, u32[]{:S(2)}) collective-permute-start(f32[16,512]{1,0:T(8,128)S(1)} %reduce_sum.18), channel_id=1, source_target_pairs={{0,256},{16,272},{32,257},{48,273},{64,258},{80,274},{96,259},{112... | collective-permute-start | bytes 98312 | tf_op jit(solution)/shard_map/ppermute | solution.py:48
  40.9 1.0 collective-permute-done
  42.0 21.2 %all_to_all.55 = f32[16,16,512]{2,1,0:T(8,128)S(1)} all-to-all(f32[16,16,512]{2,1,0:T(8,128)S(1)} %tile.9), channel_id=1, replica_groups={{256,288,320,352,384,416,448,480,0,32,64,96,128,160,192,224},{272,304,3..., dimensions={0} | all-to-all | bytes 1048576 | tf_op jit(solution)/shard_map/all_to_all | solution.py:15
  63.2 0.9 tile.8
  64.0 0.0 copy-start.2
  64.0 8.2 %all-to-all-start.1 = ((f32[16,16,512]{2,1,0:T(8,128)}), f32[16,16,512]{2,1,0:T(8,128)S(1)}, u32[]{:S(2)}, u32[]{:S(2)}) async-start(f32[16,16,512]{2,1,0:T(8,128)} %tile.8), calls=%async_computation.1 | async-start | bytes 1048576 | tf_op jit(solution)/shard_map/all_to_all | solution.py:15
  72.2 3.5 %collective-permute-start.1 = (f32[256,512]{1,0:T(8,128)S(1)}, f32[256,512]{1,0:T(8,128)S(1)}, u32[]{:S(2)}, u32[]{:S(2)}) collective-permute-start(f32[256,512]{1,0:T(8,128)S(1)} %bitcast.14), channel_id=1, source_target_pairs={{0,16},{16,0},{32,48},{48,32},{64,80},{80,64},{96,112},{112,96},{1... | collective-permute-start | bytes 1572872 | tf_op jit(solution)/shard_map/ppermute | solution.py:51
  75.7 13.2 %all-to-all-done.1 = f32[16,16,512]{2,1,0:T(8,128)S(1)} async-done(((f32[16,16,512]{2,1,0:T(8,128)}), f32[16,16,512]{2,1,0:T(8,128)S(1)}, u32[]{:S(2)}, u32[]{:S(2)}) %all-to-all-start.1) | async-done | bytes 524320 | tf_op jit(solution)/shard_map/all_to_all | solution.py:15
  88.9 0.0 collective-permute-done.1
  88.9 0.0 copy-done.2
  89.0 0.0 copy-start.1
  89.0 0.6 convolution_divide_fusion.1
  89.6 0.6 copy-done.1
  90.2 0.6 fusion.1
  90.8 21.0 %all_to_all.56 = f32[16,16,512]{2,1,0:T(8,128)S(1)} all-to-all(f32[16,16,512]{2,1,0:T(8,128)S(1)} %bitcast.12), channel_id=1, replica_groups=mesh['row'=32,'col'=16] {'col'}, dimensions={0} | all-to-all | bytes 1048576 | tf_op jit(solution)/shard_map/all_to_all | solution.py:15
  111.8 1.9 %collective-permute-start.2 = (f32[16,512]{1,0:T(8,128)S(1)}, f32[16,512]{1,0:T(8,128)S(1)}, u32[]{:S(2)}, u32[]{:S(2)}) collective-permute-start(f32[16,512]{1,0:T(8,128)S(1)} %reduce_sum.19), channel_id=1, source_target_pairs={{0,256},{16,272},{32,257},{48,273},{64,258},{80,274},{96,259},{112... | collective-permute-start | bytes 98312 | tf_op jit(solution)/shard_map/ppermute | solution.py:48
  113.7 6.6 %collective-permute-done.2 = f32[16,512]{1,0:T(8,128)S(1)} collective-permute-done((f32[16,512]{1,0:T(8,128)S(1)}, f32[16,512]{1,0:T(8,128)S(1)}, u32[]{:S(2)}, u32[]{:S(2)}) %collective-permute-start.2) | collective-permute-done | bytes 32800 | tf_op jit(solution)/shard_map/ppermute | solution.py:48
  120.4 19.5 %all_to_all.57 = f32[16,16,512]{2,1,0:T(8,128)S(1)} all-to-all(f32[16,16,512]{2,1,0:T(8,128)S(1)} %tile.11), channel_id=1, replica_groups={{256,288,320,352,384,416,448,480,0,32,64,96,128,160,192,224},{272,304,3..., dimensions={0} | all-to-all | bytes 1048576 | tf_op jit(solution)/shard_map/all_to_all | solution.py:15
  139.9 0.9 tile.10
  140.8 8.5 %all-to-all-start.4 = ((f32[16,16,512]{2,1,0:T(8,128)}), f32[16,16,512]{2,1,0:T(8,128)S(1)}, u32[]{:S(2)}, u32[]{:S(2)}) async-start(f32[16,16,512]{2,1,0:T(8,128)} %tile.10), calls=%async_computation.4 | async-start | bytes 1048576 | tf_op jit(solution)/shard_map/all_to_all | solution.py:15
  149.2 3.5 %collective-permute-start.3 = (f32[256,512]{1,0:T(8,128)S(1)}, f32[256,512]{1,0:T(8,128)S(1)}, u32[]{:S(2)}, u32[]{:S(2)}) collective-permute-start(f32[256,512]{1,0:T(8,128)S(1)} %bitcast.16), channel_id=1, source_target_pairs={{0,16},{16,0},{32,48},{48,32},{64,80},{80,64},{96,112},{112,96},{1... | collective-permute-start | bytes 1572872 | tf_op jit(solution)/shard_map/ppermute | solution.py:51
  152.7 13.3 %all-to-all-done.4 = f32[16,16,512]{2,1,0:T(8,128)S(1)} async-done(((f32[16,16,512]{2,1,0:T(8,128)}), f32[16,16,512]{2,1,0:T(8,128)S(1)}, u32[]{:S(2)}, u32[]{:S(2)}) %all-to-all-start.4) | async-done | bytes 524320 | tf_op jit(solution)/shard_map/all_to_all | solution.py:15
  166.0 0.0 collective-permute-done.3
  166.0 1.4 convolution_divide_fusion
  (4 shorter events, 0.2 us)
Async XLA Ops:
  0.0 1.0 copy-start
  30.3 11.6 %collective-permute-start = (f32[16,512]{1,0:T(8,128)S(1)}, f32[16,512]{1,0:T(8,128)S(1)}, u32[]{:S(2)}, u32[]{:S(2)}) collective-permute-start(f32[16,512]{1,0:T(8,128)S(1)} %reduce_sum.18), channel_id=1, source_target_pairs={{0,256},{16,272},{32,257},{48,273},{64,258},{80,274},{96,259},{112... | collective-permute-start | bytes 98312 | tf_op jit(solution)/shard_map/ppermute | solution.py:48
  64.0 24.9 %copy-start.2 = (f32[256,512]{1,0:T(8,128)S(1)}, f32[256,512]{1,0:T(8,128)}, u32[]{:S(2)}) copy-start(f32[256,512]{1,0:T(8,128)} %param.5) | copy-start | bytes 1572868
  64.0 24.9 %all-to-all-start.1 = ((f32[16,16,512]{2,1,0:T(8,128)}), f32[16,16,512]{2,1,0:T(8,128)S(1)}, u32[]{:S(2)}, u32[]{:S(2)}) async-start(f32[16,16,512]{2,1,0:T(8,128)} %tile.8), calls=%async_computation.1 | async-start | bytes 1048576 | tf_op jit(solution)/shard_map/all_to_all | solution.py:15
  72.2 16.8 %collective-permute-start.1 = (f32[256,512]{1,0:T(8,128)S(1)}, f32[256,512]{1,0:T(8,128)S(1)}, u32[]{:S(2)}, u32[]{:S(2)}) collective-permute-start(f32[256,512]{1,0:T(8,128)S(1)} %bitcast.14), channel_id=1, source_target_pairs={{0,16},{16,0},{32,48},{48,32},{64,80},{80,64},{96,112},{112,96},{1... | collective-permute-start | bytes 1572872 | tf_op jit(solution)/shard_map/ppermute | solution.py:51
  89.0 1.2 copy-start.1
  111.8 8.6 %collective-permute-start.2 = (f32[16,512]{1,0:T(8,128)S(1)}, f32[16,512]{1,0:T(8,128)S(1)}, u32[]{:S(2)}, u32[]{:S(2)}) collective-permute-start(f32[16,512]{1,0:T(8,128)S(1)} %reduce_sum.19), channel_id=1, source_target_pairs={{0,256},{16,272},{32,257},{48,273},{64,258},{80,274},{96,259},{112... | collective-permute-start | bytes 98312 | tf_op jit(solution)/shard_map/ppermute | solution.py:48
  140.8 25.3 %all-to-all-start.4 = ((f32[16,16,512]{2,1,0:T(8,128)}), f32[16,16,512]{2,1,0:T(8,128)S(1)}, u32[]{:S(2)}, u32[]{:S(2)}) async-start(f32[16,16,512]{2,1,0:T(8,128)} %tile.10), calls=%async_computation.4 | async-start | bytes 1048576 | tf_op jit(solution)/shard_map/all_to_all | solution.py:15
  149.2 16.8 %collective-permute-start.3 = (f32[256,512]{1,0:T(8,128)S(1)}, f32[256,512]{1,0:T(8,128)S(1)}, u32[]{:S(2)}, u32[]{:S(2)}) collective-permute-start(f32[256,512]{1,0:T(8,128)S(1)} %bitcast.16), channel_id=1, source_target_pairs={{0,16},{16,0},{32,48},{48,32},{64,80},{80,64},{96,112},{112,96},{1... | collective-permute-start | bytes 1572872 | tf_op jit(solution)/shard_map/ppermute | solution.py:51

commit v6 on v5

--- a/solution.py
+++ b/solution.py
@@ -30,9 +30,10 @@
     mine = lax.dynamic_slice_in_dim(factor, here_row % CORES * rows, rows, 0)
     mine = jnp.where(here_row // CORES == here_col, mine, 0.0)
     partner = [(r, r ^ 1) for r in range(nrow)]
+    along_yu = [[y * PAIR + u for u in range(PAIR) for y in range(line)]]
     turn = []
     along_zv = [[] for _ in range(CORES)]
-    for c in range(ncol):
+    for c in along_yu[0]:
         place = (c // PAIR + line // 2) % line * PAIR + c % PAIR
         for e in range(CORES):
             along_zv[e].append(place * CORES + e)
@@ -42,9 +43,9 @@
     amp = amplitudes
     for _ in range(ITERS):
         part = jnp.dot(amp, factor, precision=PRECISION) * scale + mine
-        terms = spread(part, "col", None)
+        terms = spread(part, "col", along_yu)
         piece = terms.reshape(ncol, rows // ncol, depth).sum(0)
-        z_rows = spread(jnp.tile(piece, (ncol, 1)), "col", None)
+        z_rows = spread(jnp.tile(piece, (ncol, 1)), "col", along_yu)
         turned = lax.ppermute(piece, ("row", "col"), turn)
         copies = jnp.tile(turned, (ncol, 1))
         col_half = spread(copies, "row", along_zv)

time: 168 us -> 160 us (0.952)
  the two profiles are of different devices: /device:TPU:1 before, /device:TPU:8 now
where the time goes in v6:
time: 160 us; the launch traced here: 159 us
  blocking collectives  84.2 us (53%)
  starting transfers between devices  35.6 us (22%)
  waiting for transfers between devices  31.1 us (19%)
  matrix products  4.72 us (3%)
  local copies, waits for them, and re-layouts  3.45 us (2%)
    all_to_all x4, blocking collectives, spread(): lax.all_to_all(block, axis, split_axis=0, concat_axis=0, axis_index_group...  84.2 us
    all_to_all x2, waiting for transfers between devices, spread(): lax.all_to_all(block, axis, split_axis=0, concat_axis=0, axis_index_group...  24.9 us
    ppermute x2, starting transfers between devices, local(): turned = lax.ppermute(piece, ('row', 'col'), turn)  16.4 us
    all_to_all x2, starting transfers between devices, spread(): lax.all_to_all(block, axis, split_axis=0, concat_axis=0, axis_index_group...  15.4 us
    ppermute x2, waiting for transfers between devices, local(): turned = lax.ppermute(piece, ('row', 'col'), turn)  6.17 us
    ppermute x2, starting transfers between devices, local(): col_rest = lax.ppermute(col_half, 'row', partner)  3.82 us
  transfers between devices with their start and end apart: 6, of which 4 were waited for; matrix products, arithmetic and copies ran while one was open for 0% of the time, Pallas kernels for 0%

profile of v6, /device:TPU:8, one launch (start us, length us, event | category | flops | bytes accessed | tf_op | source)
XLA Modules:
  0.0 159.2 jit_solution(7027642577116245069)
XLA Ops:
  0.0 0.0 copy-start
  0.0 1.0 copy-done
  1.0 2.1 %fusion = f32[256,512]{1,0:T(8,128)S(1)} fusion(f32[256,512]{1,0:T(8,128)S(1)} %copy-done, f32[512,512]{1,0:T(8,128)} %param.4, s32[]{:T(128)S(6)} %select_n.39, pred[]{:T(512)S(6)} %eq.9), kind=kOutput, calls=%fused_computation.4 | convolution fusion | flops 403046400 | bytes 2621445 | tf_op jit(solution)/shard_map/dot_general | solution.py:45
  3.1 26.1 %all_to_all.54 = f32[16,16,512]{2,1,0:T(8,128)S(1)} all-to-all(f32[16,16,512]{2,1,0:T(8,128)S(1)} %bitcast.13), channel_id=1, replica_groups={{0,2,4,6,8,10,12,14,1,3,5,7,9,11,13,15},{16,18,20,22,24,26,28,30,17,19,..., dimensions={0} | all-to-all | bytes 1048576 | tf_op jit(solution)/shard_map/all_to_all | solution.py:15
  29.2 11.3 %collective-permute-start = (f32[16,512]{1,0:T(8,128)S(1)}, f32[16,512]{1,0:T(8,128)S(1)}, u32[]{:S(2)}, u32[]{:S(2)}) collective-permute-start(f32[16,512]{1,0:T(8,128)S(1)} %reduce_sum.18), channel_id=1, source_target_pairs={{0,256},{16,272},{32,257},{48,273},{64,258},{80,274},{96,259},{112... | collective-permute-start | bytes 98312 | tf_op jit(solution)/shard_map/ppermute | solution.py:49
  40.5 1.6 collective-permute-done
  42.1 20.8 %all_to_all.55 = f32[16,16,512]{2,1,0:T(8,128)S(1)} all-to-all(f32[16,16,512]{2,1,0:T(8,128)S(1)} %tile.9), channel_id=1, replica_groups={{256,320,384,448,0,64,128,192,288,352,416,480,32,96,160,224},{272,336,4..., dimensions={0} | all-to-all | bytes 1048576 | tf_op jit(solution)/shard_map/all_to_all | solution.py:15
  62.9 0.9 tile.8
  63.8 0.0 copy-start.2
  63.8 7.9 %all-to-all-start.1 = ((f32[16,16,512]{2,1,0:T(8,128)}), f32[16,16,512]{2,1,0:T(8,128)S(1)}, u32[]{:S(2)}, u32[]{:S(2)}) async-start(f32[16,16,512]{2,1,0:T(8,128)} %tile.8), calls=%async_computation.1 | async-start | bytes 1048576 | tf_op jit(solution)/shard_map/all_to_all | solution.py:15
  71.6 1.9 %collective-permute-start.1 = (f32[256,512]{1,0:T(8,128)S(1)}, f32[256,512]{1,0:T(8,128)S(1)}, u32[]{:S(2)}, u32[]{:S(2)}) collective-permute-start(f32[256,512]{1,0:T(8,128)S(1)} %bitcast.14), channel_id=1, source_target_pairs={{0,16},{16,0},{32,48},{48,32},{64,80},{80,64},{96,112},{112,96},{1... | collective-permute-start | bytes 1572872 | tf_op jit(solution)/shard_map/ppermute | solution.py:52
  73.5 12.7 %all-to-all-done.1 = f32[16,16,512]{2,1,0:T(8,128)S(1)} async-done(((f32[16,16,512]{2,1,0:T(8,128)}), f32[16,16,512]{2,1,0:T(8,128)S(1)}, u32[]{:S(2)}, u32[]{:S(2)}) %all-to-all-start.1) | async-done | bytes 524320 | tf_op jit(solution)/shard_map/all_to_all | solution.py:15
  86.2 0.0 collective-permute-done.1
  86.2 0.0 copy-done.2
  86.2 0.0 copy-start.1
  86.2 0.6 convolution_divide_fusion.1
  86.8 0.6 copy-done.1
  87.4 0.6 fusion.1
  88.0 20.1 %all_to_all.56 = f32[16,16,512]{2,1,0:T(8,128)S(1)} all-to-all(f32[16,16,512]{2,1,0:T(8,128)S(1)} %bitcast.12), channel_id=1, replica_groups={{0,2,4,6,8,10,12,14,1,3,5,7,9,11,13,15},{16,18,20,22,24,26,28,30,17,19,..., dimensions={0} | all-to-all | bytes 1048576 | tf_op jit(solution)/shard_map/all_to_all | solution.py:15
  108.2 5.1 %collective-permute-start.2 = (f32[16,512]{1,0:T(8,128)S(1)}, f32[16,512]{1,0:T(8,128)S(1)}, u32[]{:S(2)}, u32[]{:S(2)}) collective-permute-start(f32[16,512]{1,0:T(8,128)S(1)} %reduce_sum.19), channel_id=1, source_target_pairs={{0,256},{16,272},{32,257},{48,273},{64,258},{80,274},{96,259},{112... | collective-permute-start | bytes 98312 | tf_op jit(solution)/shard_map/ppermute | solution.py:49
  113.3 4.6 %collective-permute-done.2 = f32[16,512]{1,0:T(8,128)S(1)} collective-permute-done((f32[16,512]{1,0:T(8,128)S(1)}, f32[16,512]{1,0:T(8,128)S(1)}, u32[]{:S(2)}, u32[]{:S(2)}) %collective-permute-start.2) | collective-permute-done | bytes 32800 | tf_op jit(solution)/shard_map/ppermute | solution.py:49
  118.0 17.3 %all_to_all.57 = f32[16,16,512]{2,1,0:T(8,128)S(1)} all-to-all(f32[16,16,512]{2,1,0:T(8,128)S(1)} %tile.11), channel_id=1, replica_groups={{256,320,384,448,0,64,128,192,288,352,416,480,32,96,160,224},{272,336,4..., dimensions={0} | all-to-all | bytes 1048576 | tf_op jit(solution)/shard_map/all_to_all | solution.py:15
  135.3 0.9 tile.10
  136.1 7.5 %all-to-all-start.4 = ((f32[16,16,512]{2,1,0:T(8,128)}), f32[16,16,512]{2,1,0:T(8,128)S(1)}, u32[]{:S(2)}, u32[]{:S(2)}) async-start(f32[16,16,512]{2,1,0:T(8,128)} %tile.10), calls=%async_computation.4 | async-start | bytes 1048576 | tf_op jit(solution)/shard_map/all_to_all | solution.py:15
  143.6 1.9 %collective-permute-start.3 = (f32[256,512]{1,0:T(8,128)S(1)}, f32[256,512]{1,0:T(8,128)S(1)}, u32[]{:S(2)}, u32[]{:S(2)}) collective-permute-start(f32[256,512]{1,0:T(8,128)S(1)} %bitcast.16), channel_id=1, source_target_pairs={{0,16},{16,0},{32,48},{48,32},{64,80},{80,64},{96,112},{112,96},{1... | collective-permute-start | bytes 1572872 | tf_op jit(solution)/shard_map/ppermute | solution.py:52
  145.6 12.2 %all-to-all-done.4 = f32[16,16,512]{2,1,0:T(8,128)S(1)} async-done(((f32[16,16,512]{2,1,0:T(8,128)}), f32[16,16,512]{2,1,0:T(8,128)S(1)}, u32[]{:S(2)}, u32[]{:S(2)}) %all-to-all-start.4) | async-done | bytes 524320 | tf_op jit(solution)/shard_map/all_to_all | solution.py:15
  157.8 0.0 collective-permute-done.3
  157.8 1.4 convolution_divide_fusion
  (4 shorter events, 0.2 us)
Async XLA Ops:
  0.0 1.0 copy-start
  29.2 12.9 %collective-permute-start = (f32[16,512]{1,0:T(8,128)S(1)}, f32[16,512]{1,0:T(8,128)S(1)}, u32[]{:S(2)}, u32[]{:S(2)}) collective-permute-start(f32[16,512]{1,0:T(8,128)S(1)} %reduce_sum.18), channel_id=1, source_target_pairs={{0,256},{16,272},{32,257},{48,273},{64,258},{80,274},{96,259},{112... | collective-permute-start | bytes 98312 | tf_op jit(solution)/shard_map/ppermute | solution.py:49
  63.8 22.4 %copy-start.2 = (f32[256,512]{1,0:T(8,128)S(1)}, f32[256,512]{1,0:T(8,128)}, u32[]{:S(2)}) copy-start(f32[256,512]{1,0:T(8,128)} %param.5) | copy-start | bytes 1572868
  63.8 22.4 %all-to-all-start.1 = ((f32[16,16,512]{2,1,0:T(8,128)}), f32[16,16,512]{2,1,0:T(8,128)S(1)}, u32[]{:S(2)}, u32[]{:S(2)}) async-start(f32[16,16,512]{2,1,0:T(8,128)} %tile.8), calls=%async_computation.1 | async-start | bytes 1048576 | tf_op jit(solution)/shard_map/all_to_all | solution.py:15
  71.6 14.6 %collective-permute-start.1 = (f32[256,512]{1,0:T(8,128)S(1)}, f32[256,512]{1,0:T(8,128)S(1)}, u32[]{:S(2)}, u32[]{:S(2)}) collective-permute-start(f32[256,512]{1,0:T(8,128)S(1)} %bitcast.14), channel_id=1, source_target_pairs={{0,16},{16,0},{32,48},{48,32},{64,80},{80,64},{96,112},{112,96},{1... | collective-permute-start | bytes 1572872 | tf_op jit(solution)/shard_map/ppermute | solution.py:52
  86.2 1.2 copy-start.1
  108.2 9.7 %collective-permute-start.2 = (f32[16,512]{1,0:T(8,128)S(1)}, f32[16,512]{1,0:T(8,128)S(1)}, u32[]{:S(2)}, u32[]{:S(2)}) collective-permute-start(f32[16,512]{1,0:T(8,128)S(1)} %reduce_sum.19), channel_id=1, source_target_pairs={{0,256},{16,272},{32,257},{48,273},{64,258},{80,274},{96,259},{112... | collective-permute-start | bytes 98312 | tf_op jit(solution)/shard_map/ppermute | solution.py:49
  136.1 21.7 %all-to-all-start.4 = ((f32[16,16,512]{2,1,0:T(8,128)}), f32[16,16,512]{2,1,0:T(8,128)S(1)}, u32[]{:S(2)}, u32[]{:S(2)}) async-start(f32[16,16,512]{2,1,0:T(8,128)} %tile.10), calls=%async_computation.4 | async-start | bytes 1048576 | tf_op jit(solution)/shard_map/all_to_all | solution.py:15
  143.6 14.2 %collective-permute-start.3 = (f32[256,512]{1,0:T(8,128)S(1)}, f32[256,512]{1,0:T(8,128)S(1)}, u32[]{:S(2)}, u32[]{:S(2)}) collective-permute-start(f32[256,512]{1,0:T(8,128)S(1)} %bitcast.16), channel_id=1, source_target_pairs={{0,16},{16,0},{32,48},{48,32},{64,80},{80,64},{96,112},{112,96},{1... | collective-permute-start | bytes 1572872 | tf_op jit(solution)/shard_map/ppermute | solution.py:52

commit v7 on v5

v7 whole, which is shorter than its diff:
```python
import math

import jax
import jax.numpy as jnp
from jax import lax
from jax.sharding import PartitionSpec as P

ITERS = 2
PRECISION = lax.Precision.HIGH
PAIR = 2
CORES = 2


def spread(block, axis, groups):
    return lax.all_to_all(block, axis, split_axis=0, concat_axis=0, axis_index_groups=groups, tiled=True)


def local(amplitudes, factor, denominators):
    rows, depth = amplitudes.shape[0], factor.shape[1]
    nrow = lax.axis_size("row")
    ncol = lax.axis_size("col")
    line = ncol // PAIR
    thin = rows // ncol
    here_row = lax.axis_index("row")
    here_col = lax.axis_index("col")
    first = here_row % CORES == 0
    scale = 1.0 / math.sqrt(rows * nrow)
    mine = lax.dynamic_slice_in_dim(factor, here_row % CORES * rows, rows, 0)
    mine = jnp.where(here_row // CORES == here_col, mine, 0.0)
    team = [[k * CORES + e for e in range(CORES)] for k in range(ncol)]
    partner = [(r, r ^ 1) for r in range(nrow)]
    order = [y * PAIR + u for u in range(PAIR) for y in range(line)]
    place = [(c // PAIR + line // 2) % line * PAIR + c % PAIR for c in order]
    turn = []
    for c, q in zip(order, place):
        for k in range(ncol):
            turn.append(((k * CORES + 1) * ncol + c, (q * CORES + 1) * ncol + k))
    both = [[k * CORES * ncol + c for c in order] for k in range(ncol)]
    both += [[(q * CORES + 1) * ncol + c for q in place] for c in range(ncol)]
    amp = amplitudes
    for step in range(ITERS):
        part = jnp.dot(amp, factor, precision=PRECISION) * scale + mine
        terms = spread(part, "col", [order])
        piece = terms.reshape(ncol, thin, depth).sum(0)
        pieces = lax.all_gather(piece, "row", axis=0, axis_index_groups=team, tiled=True)
        turned = lax.ppermute(pieces, ("row", "col"), turn)
        own = jnp.where(first, pieces, turned)
        got = spread(jnp.tile(own, (ncol, 1)), ("row", "col"), both)
        other = lax.ppermute(got, "row", partner)
        got = got.reshape(ncol, CORES, thin, depth)
        other = other.reshape(ncol, CORES, thin, depth)
        z_rows = jnp.where(first, got[:, 0], other[:, 1]).reshape(rows, depth)
        z_cols = jnp.where(first, other, got).transpose(1, 0, 2, 3).reshape(CORES * rows, depth)
        full = lax.dot_general(z_rows, z_cols, (((1,), (1,)), ((), ())), precision=PRECISION)
        amp = full / denominators
    return amp


def solution(mesh):
    return jax.shard_map(
        local,
        mesh=mesh,
        in_specs=(P("row", "col"), P("col", None), P("row", "col")),
        out_specs=P("row", "col"),
        check_vma=False,
    )
```

time: 168 us -> 144 us (0.86)
  waiting for transfers between devices: 34.2 us -> 10.9 us
  starting transfers between devices: 36.2 us -> 19.3 us
  blocking collectives: 88.8 us -> 104 us
    all_to_all x2 -> x0, waiting for transfers between devices: 26.5 us -> none  [spread(): lax.all_to_all(block, axis, split_axis=0, concat_axis=0, axis_index_group...]
    all_to_all x2 -> x0, starting transfers between devices: 16.6 us -> none  [spread(): lax.all_to_all(block, axis, split_axis=0, concat_axis=0, axis_index_group...]
    all_gather x0 -> x2, blocking collectives: none -> 8.71 us  [local(): lax.all_gather(piece, 'row', axis=0, axis_index_groups=team, tiled=True)]
    all_to_all x4, blocking collectives: 88.8 us -> 95.7 us  [spread(): lax.all_to_all(block, axis, split_axis=0, concat_axis=0, axis_index_group...]
    ppermute x4, waiting for transfers between devices: 7.65 us -> 10.9 us  [the longest x2 5.68 us: local(): turned = lax.ppermute(pieces, ('row', 'col'), turn)]
  transfers between devices with their start and end apart: 6 -> 4, of which waited for: 4 -> 4; matrix products, arithmetic and copies ran while one was open for 0% -> 0% of each run, Pallas kernels for 0% -> 0%
where the time goes in v7:
time: 144 us; the launch traced here: 143 us
  blocking collectives  104 us (72%)
  starting transfers between devices  19.3 us (13%)
  waiting for transfers between devices  10.9 us (8%)
  matrix products  4.65 us (3%)
  local copies, waits for them, and re-layouts  2.96 us (2%)
    all_to_all x4, blocking collectives, spread(): lax.all_to_all(block, axis, split_axis=0, concat_axis=0, axis_index_group...  95.7 us
    ppermute x2, starting transfers between devices, local(): turned = lax.ppermute(pieces, ('row', 'col'), turn)  15.5 us
    all_gather x2, blocking collectives, local(): lax.all_gather(piece, 'row', axis=0, axis_index_groups=team, tiled=True)  8.71 us
    ppermute x2, waiting for transfers between devices, local(): turned = lax.ppermute(pieces, ('row', 'col'), turn)  5.68 us
    ppermute x2, waiting for transfers between devices, local(): other = lax.ppermute(got, 'row', partner)  5.25 us
    ppermute x2, starting transfers between devices, local(): other = lax.ppermute(got, 'row', partner)  3.82 us
  transfers between devices with their start and end apart: 4, of which 4 were waited for; matrix products, arithmetic and copies ran while one was open for 0% of the time, Pallas kernels for 0%

profile of v7, /device:TPU:1, one launch (start us, length us, event | category | flops | bytes accessed | tf_op | source)
XLA Modules:
  0.0 143.2 jit_solution(9374795697926988919)
XLA Ops:
  0.0 0.0 copy-start
  0.0 1.0 copy-done
  1.0 2.0 %fusion = f32[256,512]{1,0:T(8,128)S(1)} fusion(f32[256,512]{1,0:T(8,128)S(1)} %copy-done, f32[512,512]{1,0:T(8,128)} %param.4, s32[]{:T(128)S(6)} %select_n.73, pred[]{:T(512)S(6)} %eq.10), kind=kOutput, calls=%fused_computation.4 | convolution fusion | flops 403046400 | bytes 2621445 | tf_op jit(solution)/shard_map/dot_general | solution.py:42
  3.0 25.0 %all_to_all.36 = f32[16,16,512]{2,1,0:T(8,128)S(1)} all-to-all(f32[16,16,512]{2,1,0:T(8,128)S(1)} %bitcast.39), channel_id=1, replica_groups={{0,2,4,6,8,10,12,14,1,3,5,7,9,11,13,15},{16,18,20,22,24,26,28,30,17,19,..., dimensions={0} | all-to-all | bytes 1048576 | tf_op jit(solution)/shard_map/all_to_all | solution.py:15
  28.1 4.6 %all_gather.6 = f32[32,512]{1,0:T(8,128)S(1)} all-gather(f32[16,512]{1,0:T(8,128)S(1)} %reduce_sum.18), channel_id=1, replica_groups={{0,16},{32,48},{64,80},{96,112},{128,144},{160,176},{192,208},{224,240}..., dimensions={0}, use_global_device_ids=true | all-gather | bytes 98304 | tf_op jit(solution)/shard_map/all_gather | solution.py:45
  32.7 10.6 %collective-permute-start = (f32[32,512]{1,0:T(8,128)S(1)}, f32[32,512]{1,0:T(8,128)S(1)}, u32[]{:S(2)}, u32[]{:S(2)}) collective-permute-start(f32[32,512]{1,0:T(8,128)S(1)} %all_gather.6), channel_id=1, source_target_pairs={{16,272},{48,273},{80,274},{112,275},{144,276},{176,277},{208,278}... | collective-permute-start | bytes 196616 | tf_op jit(solution)/shard_map/ppermute | solution.py:46
  43.3 1.3 collective-permute-done
  44.7 0.1 tile.4
  44.8 26.4 %all_to_all.37 = f32[16,32,512]{2,1,0:T(8,128)S(1)} all-to-all(f32[16,32,512]{2,1,0:T(8,128)S(1)} %tile.4), channel_id=1, replica_groups={{0,2,4,6,8,10,12,14,1,3,5,7,9,11,13,15},{32,34,36,38,40,42,44,46,33,35,..., dimensions={0} | all-to-all | bytes 2097152 | tf_op jit(solution)/shard_map/all_to_all | solution.py:15
  71.2 1.9 %collective-permute-start.1 = (f32[512,512]{1,0:T(8,128)S(1)}, f32[512,512]{1,0:T(8,128)S(1)}, u32[]{:S(2)}, u32[]{:S(2)}) collective-permute-start(f32[512,512]{1,0:T(8,128)S(1)} %bitcast.27), channel_id=1, source_target_pairs={{0,16},{16,0},{32,48},{48,32},{64,80},{80,64},{96,112},{112,96},{1... | collective-permute-start | bytes 3145736 | tf_op jit(solution)/shard_map/ppermute | solution.py:49
  73.1 2.6 %collective-permute-done.1 = f32[512,512]{1,0:T(8,128)S(1)} collective-permute-done((f32[512,512]{1,0:T(8,128)S(1)}, f32[512,512]{1,0:T(8,128)S(1)}, u32[]{:S(2)}, u32[]{:S(2)}) %collective-permute-start.1) | collective-permute-done | bytes 1048608 | tf_op jit(solution)/shard_map/ppermute | solution.py:49
  75.8 0.1 slice_select_fusion.1
  75.8 0.3 select_bitcast_fusion.1
  76.1 0.0 copy-start.2
  76.1 0.1 copy.4
  76.2 1.0 copy-done.2
  77.2 0.0 copy-start.1
  77.2 0.6 convolution_divide_fusion.1
  77.8 0.6 copy-done.1
  78.4 0.6 fusion.1
  79.0 21.7 %all_to_all.38 = f32[16,16,512]{2,1,0:T(8,128)S(1)} all-to-all(f32[16,16,512]{2,1,0:T(8,128)S(1)} %bitcast.38), channel_id=1, replica_groups={{0,2,4,6,8,10,12,14,1,3,5,7,9,11,13,15},{16,18,20,22,24,26,28,30,17,19,..., dimensions={0} | all-to-all | bytes 1048576 | tf_op jit(solution)/shard_map/all_to_all | solution.py:15
  100.7 4.1 %all_gather.7 = f32[32,512]{1,0:T(8,128)S(1)} all-gather(f32[16,512]{1,0:T(8,128)S(1)} %reduce_sum.19), channel_id=1, replica_groups={{0,16},{32,48},{64,80},{96,112},{128,144},{160,176},{192,208},{224,240}..., dimensions={0}, use_global_device_ids=true | all-gather | bytes 98304 | tf_op jit(solution)/shard_map/all_gather | solution.py:45
  104.8 4.9 %collective-permute-start.2 = (f32[32,512]{1,0:T(8,128)S(1)}, f32[32,512]{1,0:T(8,128)S(1)}, u32[]{:S(2)}, u32[]{:S(2)}) collective-permute-start(f32[32,512]{1,0:T(8,128)S(1)} %all_gather.7), channel_id=1, source_target_pairs={{16,272},{48,273},{80,274},{112,275},{144,276},{176,277},{208,278}... | collective-permute-start | bytes 196616 | tf_op jit(solution)/shard_map/ppermute | solution.py:46
  109.7 4.3 %collective-permute-done.2 = f32[32,512]{1,0:T(8,128)S(1)} collective-permute-done((f32[32,512]{1,0:T(8,128)S(1)}, f32[32,512]{1,0:T(8,128)S(1)}, u32[]{:S(2)}, u32[]{:S(2)}) %collective-permute-start.2) | collective-permute-done | bytes 65568 | tf_op jit(solution)/shard_map/ppermute | solution.py:46
  114.0 0.1 tile.5
  114.2 22.6 %all_to_all.39 = f32[16,32,512]{2,1,0:T(8,128)S(1)} all-to-all(f32[16,32,512]{2,1,0:T(8,128)S(1)} %tile.5), channel_id=1, replica_groups={{0,2,4,6,8,10,12,14,1,3,5,7,9,11,13,15},{32,34,36,38,40,42,44,46,33,35,..., dimensions={0} | all-to-all | bytes 2097152 | tf_op jit(solution)/shard_map/all_to_all | solution.py:15
  136.8 1.9 %collective-permute-start.3 = (f32[512,512]{1,0:T(8,128)S(1)}, f32[512,512]{1,0:T(8,128)S(1)}, u32[]{:S(2)}, u32[]{:S(2)}) collective-permute-start(f32[512,512]{1,0:T(8,128)S(1)} %bitcast.24), channel_id=1, source_target_pairs={{0,16},{16,0},{32,48},{48,32},{64,80},{80,64},{96,112},{112,96},{1... | collective-permute-start | bytes 3145736 | tf_op jit(solution)/shard_map/ppermute | solution.py:49
  138.7 2.6 %collective-permute-done.3 = f32[512,512]{1,0:T(8,128)S(1)} collective-permute-done((f32[512,512]{1,0:T(8,128)S(1)}, f32[512,512]{1,0:T(8,128)S(1)}, u32[]{:S(2)}, u32[]{:S(2)}) %collective-permute-start.3) | collective-permute-done | bytes 1048608 | tf_op jit(solution)/shard_map/ppermute | solution.py:49
  141.3 0.1 slice_select_fusion
  141.4 0.3 select_bitcast_fusion
  141.7 0.1 copy.5
  141.8 1.4 convolution_divide_fusion
  (4 shorter events, 0.1 us)
Async XLA Ops:
  0.0 1.0 copy-start
  32.7 12.0 %collective-permute-start = (f32[32,512]{1,0:T(8,128)S(1)}, f32[32,512]{1,0:T(8,128)S(1)}, u32[]{:S(2)}, u32[]{:S(2)}) collective-permute-start(f32[32,512]{1,0:T(8,128)S(1)} %all_gather.6), channel_id=1, source_target_pairs={{16,272},{48,273},{80,274},{112,275},{144,276},{176,277},{208,278}... | collective-permute-start | bytes 196616 | tf_op jit(solution)/shard_map/ppermute | solution.py:46
  71.2 4.5 %collective-permute-start.1 = (f32[512,512]{1,0:T(8,128)S(1)}, f32[512,512]{1,0:T(8,128)S(1)}, u32[]{:S(2)}, u32[]{:S(2)}) collective-permute-start(f32[512,512]{1,0:T(8,128)S(1)} %bitcast.27), channel_id=1, source_target_pairs={{0,16},{16,0},{32,48},{48,32},{64,80},{80,64},{96,112},{112,96},{1... | collective-permute-start | bytes 3145736 | tf_op jit(solution)/shard_map/ppermute | solution.py:49
  76.1 1.0 copy-start.2
  77.2 1.2 copy-start.1
  104.8 9.2 %collective-permute-start.2 = (f32[32,512]{1,0:T(8,128)S(1)}, f32[32,512]{1,0:T(8,128)S(1)}, u32[]{:S(2)}, u32[]{:S(2)}) collective-permute-start(f32[32,512]{1,0:T(8,128)S(1)} %all_gather.7), channel_id=1, source_target_pairs={{16,272},{48,273},{80,274},{112,275},{144,276},{176,277},{208,278}... | collective-permute-start | bytes 196616 | tf_op jit(solution)/shard_map/ppermute | solution.py:46
  136.8 4.5 %collective-permute-start.3 = (f32[512,512]{1,0:T(8,128)S(1)}, f32[512,512]{1,0:T(8,128)S(1)}, u32[]{:S(2)}, u32[]{:S(2)}) collective-permute-start(f32[512,512]{1,0:T(8,128)S(1)} %bitcast.24), channel_id=1, source_target_pairs={{0,16},{16,0},{32,48},{48,32},{64,80},{80,64},{96,112},{112,96},{1... | collective-permute-start | bytes 3145736 | tf_op jit(solution)/shard_map/ppermute | solution.py:49

commit v8 on v7

--- a/solution.py
+++ b/solution.py
@@ -31,20 +31,23 @@
     partner = [(r, r ^ 1) for r in range(nrow)]
     order = [y * PAIR + u for u in range(PAIR) for y in range(line)]
     place = [(c // PAIR + line // 2) % line * PAIR + c % PAIR for c in order]
-    turn = []
-    for c, q in zip(order, place):
-        for k in range(ncol):
-            turn.append(((k * CORES + 1) * ncol + c, (q * CORES + 1) * ncol + k))
+    turn = [[] for _ in range(CORES)]
+    for e in range(CORES):
+        for c, q in zip(order, place):
+            for k in range(ncol):
+                turn[e].append(((k * CORES + e) * ncol + c, (q * CORES + 1) * ncol + k))
     both = [[k * CORES * ncol + c for c in order] for k in range(ncol)]
     both += [[(q * CORES + 1) * ncol + c for q in place] for c in range(ncol)]
     amp = amplitudes
-    for step in range(ITERS):
+    for _ in range(ITERS):
         part = jnp.dot(amp, factor, precision=PRECISION) * scale + mine
         terms = spread(part, "col", [order])
         piece = terms.reshape(ncol, thin, depth).sum(0)
+        turned = []
+        for e in range(CORES):
+            turned.append(lax.ppermute(piece, ("row", "col"), turn[e]))
         pieces = lax.all_gather(piece, "row", axis=0, axis_index_groups=team, tiled=True)
-        turned = lax.ppermute(pieces, ("row", "col"), turn)
-        own = jnp.where(first, pieces, turned)
+        own = jnp.where(first, pieces, jnp.concatenate(turned))
         got = spread(jnp.tile(own, (ncol, 1)), ("row", "col"), both)
         other = lax.ppermute(got, "row", partner)
         got = got.reshape(ncol, CORES, thin, depth)

time: 144 us -> 142 us (0.986)
  starting transfers between devices: 19.3 us -> 24.8 us
  waiting for transfers between devices: 10.9 us -> 7.15 us
  blocking collectives: 104 us -> 101 us
    all_to_all x4, blocking collectives: 95.7 us -> 88 us  [spread(): lax.all_to_all(block, axis, split_axis=0, concat_axis=0, axis_index_group...]
    all_gather x2, blocking collectives: 8.71 us -> 13.1 us  [local(): lax.all_gather(piece, 'row', axis=0, axis_index_groups=team, tiled=True)]
    ppermute x2 -> x4, waiting for transfers between devices: 5.68 us -> 2.62 us  [local(): turned.append(lax.ppermute(piece, ('row', 'col'), turn[e]))]
    ppermute x2, starting transfers between devices: 3.82 us -> 6.78 us  [local(): other = lax.ppermute(got, 'row', partner)]
    ppermute x2 -> x4, starting transfers between devices: 15.5 us -> 18 us  [local(): turned.append(lax.ppermute(piece, ('row', 'col'), turn[e]))]
  transfers between devices with their start and end apart: 4 -> 6, of which waited for: 4 -> 4; matrix products, arithmetic and copies ran while one was open for 0% -> 0% of each run, Pallas kernels for 0% -> 0%
where the time goes in v8:
time: 142 us
  blocking collectives  101 us (71%)
  starting transfers between devices  24.8 us (17%)
  waiting for transfers between devices  7.15 us (5%)
  matrix products  4.65 us (3%)
  local copies, waits for them, and re-layouts  2.96 us (2%)
    all_to_all x4, blocking collectives, spread(): lax.all_to_all(block, axis, split_axis=0, concat_axis=0, axis_index_group...  88 us
    ppermute x4, starting transfers between devices, local(): turned.append(lax.ppermute(piece, ('row', 'col'), turn[e]))  18 us
    all_gather x2, blocking collectives, local(): lax.all_gather(piece, 'row', axis=0, axis_index_groups=team, tiled=True)  13.1 us
    ppermute x2, starting transfers between devices, local(): other = lax.ppermute(got, 'row', partner)  6.78 us
    ppermute x2, waiting for transfers between devices, local(): other = lax.ppermute(got, 'row', partner)  4.53 us
  transfers between devices with their start and end apart: 6, of which 4 were waited for; matrix products, arithmetic and copies ran while one was open for 0% of the time, Pallas kernels for 0%

profile of v8, /device:TPU:1, one launch (start us, length us, event | category | flops | bytes accessed | tf_op | source)
XLA Modules:
  0.0 141.6 jit_solution(2005973873346451429)
XLA Ops:
  0.0 0.0 copy-start
  0.0 1.0 copy-done
  1.0 2.0 %fusion = f32[256,512]{1,0:T(8,128)S(1)} fusion(f32[256,512]{1,0:T(8,128)S(1)} %copy-done, f32[512,512]{1,0:T(8,128)} %param.4, s32[]{:T(128)S(6)} %select_n.73, pred[]{:T(512)S(6)} %eq.10), kind=kOutput, calls=%fused_computation.4 | convolution fusion | flops 403046400 | bytes 2621445 | tf_op jit(solution)/shard_map/dot_general | solution.py:43
  3.0 25.0 %all_to_all.36 = f32[16,16,512]{2,1,0:T(8,128)S(1)} all-to-all(f32[16,16,512]{2,1,0:T(8,128)S(1)} %bitcast.39), channel_id=1, replica_groups={{0,2,4,6,8,10,12,14,1,3,5,7,9,11,13,15},{16,18,20,22,24,26,28,30,17,19,..., dimensions={0} | all-to-all | bytes 1048576 | tf_op jit(solution)/shard_map/all_to_all | solution.py:15
  28.1 10.6 %collective-permute-start.1 = (f32[16,512]{1,0:T(8,128)S(1)}, f32[16,512]{1,0:T(8,128)S(1)}, u32[]{:S(2)}, u32[]{:S(2)}) collective-permute-start(f32[16,512]{1,0:T(8,128)S(1)} %reduce_sum.18), channel_id=1, source_target_pairs={{16,272},{48,273},{80,274},{112,275},{144,276},{176,277},{208,278}... | collective-permute-start | bytes 98312 | tf_op jit(solution)/shard_map/ppermute | solution.py:48
  38.7 1.3 collective-permute-start
  40.0 6.4 %all_gather.6 = f32[32,512]{1,0:T(8,128)S(1)} all-gather(f32[16,512]{1,0:T(8,128)S(1)} %reduce_sum.18), channel_id=1, replica_groups={{0,16},{32,48},{64,80},{96,112},{128,144},{160,176},{192,208},{224,240}..., dimensions={0}, use_global_device_ids=true | all-gather | bytes 98304 | tf_op jit(solution)/shard_map/all_gather | solution.py:49
  46.4 0.0 collective-permute-done.1
  46.4 1.4 %collective-permute-done = f32[16,512]{1,0:T(8,128)S(1)} collective-permute-done((f32[16,512]{1,0:T(8,128)S(1)}, f32[16,512]{1,0:T(8,128)S(1)}, u32[]{:S(2)}, u32[]{:S(2)}) %collective-permute-start) | collective-permute-done | bytes 32800 | tf_op jit(solution)/shard_map/ppermute | solution.py:48
  47.9 0.1 tile.4
  48.0 22.1 %all_to_all.37 = f32[16,32,512]{2,1,0:T(8,128)S(1)} all-to-all(f32[16,32,512]{2,1,0:T(8,128)S(1)} %tile.4), channel_id=1, replica_groups={{0,2,4,6,8,10,12,14,1,3,5,7,9,11,13,15},{32,34,36,38,40,42,44,46,33,35,..., dimensions={0} | all-to-all | bytes 2097152 | tf_op jit(solution)/shard_map/all_to_all | solution.py:15
  70.1 3.4 %collective-permute-start.2 = (f32[512,512]{1,0:T(8,128)S(1)}, f32[512,512]{1,0:T(8,128)S(1)}, u32[]{:S(2)}, u32[]{:S(2)}) collective-permute-start(f32[512,512]{1,0:T(8,128)S(1)} %bitcast.27), channel_id=1, source_target_pairs={{0,16},{16,0},{32,48},{48,32},{64,80},{80,64},{96,112},{112,96},{1... | collective-permute-start | bytes 3145736 | tf_op jit(solution)/shard_map/ppermute | solution.py:52
  73.6 2.3 %collective-permute-done.2 = f32[512,512]{1,0:T(8,128)S(1)} collective-permute-done((f32[512,512]{1,0:T(8,128)S(1)}, f32[512,512]{1,0:T(8,128)S(1)}, u32[]{:S(2)}, u32[]{:S(2)}) %collective-permute-start.2) | collective-permute-done | bytes 1048608 | tf_op jit(solution)/shard_map/ppermute | solution.py:52
  75.8 0.1 slice_select_fusion.1
  75.9 0.3 select_bitcast_fusion.1
  76.2 0.0 copy-start.2
  76.2 0.1 copy.4
  76.3 1.0 copy-done.2
  77.2 0.0 copy-start.1
  77.2 0.6 convolution_divide_fusion.1
  77.9 0.6 copy-done.1
  78.5 0.6 fusion.1
  79.1 19.3 %all_to_all.38 = f32[16,16,512]{2,1,0:T(8,128)S(1)} all-to-all(f32[16,16,512]{2,1,0:T(8,128)S(1)} %bitcast.38), channel_id=1, replica_groups={{0,2,4,6,8,10,12,14,1,3,5,7,9,11,13,15},{16,18,20,22,24,26,28,30,17,19,..., dimensions={0} | all-to-all | bytes 1048576 | tf_op jit(solution)/shard_map/all_to_all | solution.py:15
  98.4 4.8 %collective-permute-start.4 = (f32[16,512]{1,0:T(8,128)S(1)}, f32[16,512]{1,0:T(8,128)S(1)}, u32[]{:S(2)}, u32[]{:S(2)}) collective-permute-start(f32[16,512]{1,0:T(8,128)S(1)} %reduce_sum.19), channel_id=1, source_target_pairs={{16,272},{48,273},{80,274},{112,275},{144,276},{176,277},{208,278}... | collective-permute-start | bytes 98312 | tf_op jit(solution)/shard_map/ppermute | solution.py:48
  103.2 1.3 collective-permute-start.3
  104.5 6.7 %all_gather.7 = f32[32,512]{1,0:T(8,128)S(1)} all-gather(f32[16,512]{1,0:T(8,128)S(1)} %reduce_sum.19), channel_id=1, replica_groups={{0,16},{32,48},{64,80},{96,112},{128,144},{160,176},{192,208},{224,240}..., dimensions={0}, use_global_device_ids=true | all-gather | bytes 98304 | tf_op jit(solution)/shard_map/all_gather | solution.py:49
  111.2 0.0 collective-permute-done.4
  111.2 1.2 collective-permute-done.3
  112.3 0.1 tile.5
  112.5 21.6 %all_to_all.39 = f32[16,32,512]{2,1,0:T(8,128)S(1)} all-to-all(f32[16,32,512]{2,1,0:T(8,128)S(1)} %tile.5), channel_id=1, replica_groups={{0,2,4,6,8,10,12,14,1,3,5,7,9,11,13,15},{32,34,36,38,40,42,44,46,33,35,..., dimensions={0} | all-to-all | bytes 2097152 | tf_op jit(solution)/shard_map/all_to_all | solution.py:15
  134.1 3.4 %collective-permute-start.5 = (f32[512,512]{1,0:T(8,128)S(1)}, f32[512,512]{1,0:T(8,128)S(1)}, u32[]{:S(2)}, u32[]{:S(2)}) collective-permute-start(f32[512,512]{1,0:T(8,128)S(1)} %bitcast.24), channel_id=1, source_target_pairs={{0,16},{16,0},{32,48},{48,32},{64,80},{80,64},{96,112},{112,96},{1... | collective-permute-start | bytes 3145736 | tf_op jit(solution)/shard_map/ppermute | solution.py:52
  137.4 2.3 %collective-permute-done.5 = f32[512,512]{1,0:T(8,128)S(1)} collective-permute-done((f32[512,512]{1,0:T(8,128)S(1)}, f32[512,512]{1,0:T(8,128)S(1)}, u32[]{:S(2)}, u32[]{:S(2)}) %collective-permute-start.5) | collective-permute-done | bytes 1048608 | tf_op jit(solution)/shard_map/ppermute | solution.py:52
  139.7 0.1 slice_select_fusion
  139.8 0.3 select_bitcast_fusion
  140.1 0.1 copy.5
  140.1 1.4 %convolution_divide_fusion = f32[256,512]{1,0:T(8,128)} fusion(f32[256,512]{1,0:T(8,128)S(1)} %copy-done.2, f32[256,512]{1,0:T(8,128)S(1)} %bitcast.36, f32[512,512]{1,0:T(8,128)S(1)} %bitcast.31), kind=kOutput, calls=%fused_computation | convolution fusion | flops 402784256 | bytes 2621440 | tf_op jit(solution)/shard_map/dot_general | solution.py:57
  (4 shorter events, 0.1 us)
Async XLA Ops:
  0.0 1.0 copy-start
  28.1 18.3 %collective-permute-start.1 = (f32[16,512]{1,0:T(8,128)S(1)}, f32[16,512]{1,0:T(8,128)S(1)}, u32[]{:S(2)}, u32[]{:S(2)}) collective-permute-start(f32[16,512]{1,0:T(8,128)S(1)} %reduce_sum.18), channel_id=1, source_target_pairs={{16,272},{48,273},{80,274},{112,275},{144,276},{176,277},{208,278}... | collective-permute-start | bytes 98312 | tf_op jit(solution)/shard_map/ppermute | solution.py:48
  38.7 9.1 %collective-permute-start = (f32[16,512]{1,0:T(8,128)S(1)}, f32[16,512]{1,0:T(8,128)S(1)}, u32[]{:S(2)}, u32[]{:S(2)}) collective-permute-start(f32[16,512]{1,0:T(8,128)S(1)} %reduce_sum.18), channel_id=1, source_target_pairs={{0,272},{32,273},{64,274},{96,275},{128,276},{160,277},{192,278},{... | collective-permute-start | bytes 98312 | tf_op jit(solution)/shard_map/ppermute | solution.py:48
  70.1 5.7 %collective-permute-start.2 = (f32[512,512]{1,0:T(8,128)S(1)}, f32[512,512]{1,0:T(8,128)S(1)}, u32[]{:S(2)}, u32[]{:S(2)}) collective-permute-start(f32[512,512]{1,0:T(8,128)S(1)} %bitcast.27), channel_id=1, source_target_pairs={{0,16},{16,0},{32,48},{48,32},{64,80},{80,64},{96,112},{112,96},{1... | collective-permute-start | bytes 3145736 | tf_op jit(solution)/shard_map/ppermute | solution.py:52
  76.2 1.0 copy-start.2
  77.2 1.2 copy-start.1
  98.4 12.7 %collective-permute-start.4 = (f32[16,512]{1,0:T(8,128)S(1)}, f32[16,512]{1,0:T(8,128)S(1)}, u32[]{:S(2)}, u32[]{:S(2)}) collective-permute-start(f32[16,512]{1,0:T(8,128)S(1)} %reduce_sum.19), channel_id=1, source_target_pairs={{16,272},{48,273},{80,274},{112,275},{144,276},{176,277},{208,278}... | collective-permute-start | bytes 98312 | tf_op jit(solution)/shard_map/ppermute | solution.py:48
  103.2 9.2 %collective-permute-start.3 = (f32[16,512]{1,0:T(8,128)S(1)}, f32[16,512]{1,0:T(8,128)S(1)}, u32[]{:S(2)}, u32[]{:S(2)}) collective-permute-start(f32[16,512]{1,0:T(8,128)S(1)} %reduce_sum.19), channel_id=1, source_target_pairs={{0,272},{32,273},{64,274},{96,275},{128,276},{160,277},{192,278},{... | collective-permute-start | bytes 98312 | tf_op jit(solution)/shard_map/ppermute | solution.py:48
  134.1 5.6 %collective-permute-start.5 = (f32[512,512]{1,0:T(8,128)S(1)}, f32[512,512]{1,0:T(8,128)S(1)}, u32[]{:S(2)}, u32[]{:S(2)}) collective-permute-start(f32[512,512]{1,0:T(8,128)S(1)} %bitcast.24), channel_id=1, source_target_pairs={{0,16},{16,0},{32,48},{48,32},{64,80},{80,64},{96,112},{112,96},{1... | collective-permute-start | bytes 3145736 | tf_op jit(solution)/shard_map/ppermute | solution.py:52
